TPU v7x, 32 devices: a whole 2x2x4 slice. The times are simulated.
32 devices in a mesh: groups: 1, seq: 16 (over z, y, core), head: 2 (over x), dp: 1.
Axes of the slice: x: 2, y: 2, z: 4, core: 2. Of those that a mesh axis runs over, the one named last changes fastest.
Arguments:
- queries: bfloat16 [1, 4096, 1024], P(('groups', 'dp'), 'seq', 'head'), may hold values from -3 to 3
- keys_in: bfloat16 [1, 4096, 1024], P(('groups', 'dp'), 'seq', 'head'), may hold values from -3 to 3
- values: bfloat16 [1, 4096, 1024], P(('groups', 'dp'), 'seq', 'head'), may hold values from -6 to 6
- grad_out: bfloat16 [1, 4096, 1024], P(('groups', 'dp'), 'seq', 'head'), may hold values from -3 to 3
- latent: bfloat16 [1, 4096, 16], P(('groups', 'dp'), 'seq'), may hold values from -16 to 4
- gate_weight: bfloat16 [16, 8], P(None, 'head')
- gate_bias: float32 [8], P('head')
- doc_starts: int32 [1, 33], P(('groups', 'dp')), may hold values from 0 to 4096, as said below
- block_docs: int32 [1, 16], P(('groups', 'dp'), 'seq'), may hold values from 0 to 31, as said below
Outputs:
- grad_queries: bfloat16 [1, 4096, 1024], P(('groups', 'dp'), 'seq', 'head')
- grad_keys: bfloat16 [1, 4096, 1024], P(('groups', 'dp'), 'seq', 'head')
- grad_values: bfloat16 [1, 4096, 1024], P(('groups', 'dp'), 'seq', 'head')
- grad_latent: float32 [1, 4096, 16], P(('groups', 'dp'), 'seq')
- grad_gate_weight: float32 [16, 8], P('groups', 'head')
Inputs may be any that keep to these rules, and one draw needn't show every extreme that they name: `doc_starts`: row s lists the first positions of the stream's 32 documents in increasing order, beginning with 0 and followed by 4096. Entry (s, m) is the document of stream s that holds position m * 256: doc_starts[s, e] <= m * 256 < doc_starts[s, e + 1] for e = block_docs[s, m].
All inputs are finite; a program needn't handle non-finite values.
Results may differ from a plain program's by a relative error of at most 0.0095.
Values sent between devices are 32-bit elements; how exact they have to be, the bound alone decides.
A program may use at most 64 MiB of HBM per device.

v0:
```python
import functools
import math

import jax
import jax.numpy as jnp
from jax import lax
from jax.experimental import pallas as pl
from jax.experimental.pallas import tpu as pltpu
from jax.sharding import PartitionSpec as P

HEAD_DIM = 128
LANES = 128
PAIR = 2
SIDE = 2

MESH = pl.DeviceIdType.MESH
precise = lax.Precision.HIGHEST
F32 = jnp.float32
BF16 = jnp.bfloat16


def dot(left, right, over, precision=None):
    return lax.dot_general(
        left, right, (((over[0],), (over[1],)), ((), ())),
        precision=precision, preferred_element_type=F32,
    )


def halves(tensor):
    upper = tensor.astype(BF16)
    return upper, (tensor - upper.astype(F32)).astype(BF16)


def kernel(
    sizes,
    q_ref, k_ref, v_ref, g_ref, latent_ref, weight_ref, bias_ref, bounds_ref,
    gq_ref, gk_ref, gv_ref, glat_ref, gw_ref,
    rows_ref, cols_ref, iq_ref, ik_ref, iv_ref,
    t_ref, part_ref, mate_ref, agg_ref, chain_out, chain_in, side_out, side_in, back_out, state_ref,
    lat_slots, gw_slots,
    t_send, t_recv, mate_send, mate_recv, chain_send, chain_recv, side_send, side_recv,
    back_send, back_recv, lat_send, lat_recv, gw_send, gw_recv,
):
    seq_count, dp_count, head_devices, heads = sizes
    rows = q_ref.shape[0]
    half = heads // PAIR
    layer = PAIR * SIDE
    depth = seq_count // layer
    scaling = 1.0 / math.sqrt(HEAD_DIM)
    me = lax.axis_index("seq")
    my_dp = lax.axis_index("dp")
    my_head = lax.axis_index("head")
    core = lax.rem(me, PAIR)
    side = lax.rem(lax.div(me, PAIR), SIDE)
    level = lax.div(me, layer)
    group = level * layer
    mate = group + side * PAIR + (1 - core)
    across = group + (1 - side) * PAIR + core
    members = seq_count * dp_count
    flat = me * dp_count + my_dp

    def member(index):
        return {"seq": lax.div(index, dp_count), "dp": lax.rem(index, dp_count)}

    barrier = pltpu.get_barrier_semaphore()
    for away in range(1, members):
        pl.semaphore_signal(
            barrier, inc=1, device_id=member(lax.rem(flat + away, members)), device_id_type=MESH
        )
    for away in range(1, head_devices):
        pl.semaphore_signal(
            barrier, inc=1, device_id={"head": lax.rem(my_head + away, head_devices)},
            device_id_type=MESH,
        )

    gate_rows = dot(weight_ref[...], latent_ref[...], (0, 1))
    eye = lax.broadcasted_iota(jnp.int32, (heads, heads), 0) == lax.broadcasted_iota(
        jnp.int32, (heads, heads), 1
    )
    bias = jnp.sum(jnp.where(eye, bias_ref[...], 0.0), axis=1, keepdims=True)
    gate_rows = gate_rows + bias
    log_decay = (jnp.minimum(gate_rows, 0.0) - jnp.log1p(jnp.exp(-jnp.abs(gate_rows)))) / 16.0
    row_id = lax.broadcasted_iota(jnp.int32, (rows, rows), 0)
    col_id = lax.broadcasted_iota(jnp.int32, (rows, rows), 1)
    upto = (row_id <= col_id).astype(F32)
    cumul = dot(log_decay, upto, (1, 0), precise)
    first_pos = me * rows
    bounds = bounds_ref[...]
    position = first_pos + lax.broadcasted_iota(jnp.int32, (rows, bounds.shape[1]), 0)
    opened = jnp.where((bounds >= first_pos) & (bounds <= position), 1.0, 0.0).astype(BF16)
    docs = dot(jnp.ones((8, bounds.shape[1]), BF16), opened, (1, 1))
    doc_row = docs[0:1]
    doc_last = doc_row[:, rows - 1:]
    ending = cumul[:, rows - 1:]
    carry_in = jnp.where(doc_row == 0.0, jnp.exp(cumul), 0.0) * scaling
    carry_out = jnp.where(doc_row == doc_last, jnp.exp(ending - cumul), 0.0)
    through = jnp.where(doc_last == 0.0, jnp.exp(ending), 0.0)
    rows_ref[...] = jnp.zeros_like(rows_ref)
    rows_ref[0:heads] = cumul
    rows_ref[heads:2 * heads] = carry_in
    rows_ref[2 * heads:3 * heads] = carry_out
    rows_ref[3 * heads:3 * heads + 8] = docs
    cols_ref[...] = rows_ref[...].T
    own_through = jnp.broadcast_to(through, (heads, LANES))
    t_ref[core + PAIR * side, 0:heads] = own_through

    def column(index):
        return cols_ref[:, index:index + 1]

    def head_lanes(index):
        return pl.ds(index * HEAD_DIM, HEAD_DIM)

    pl.semaphore_wait(barrier, members - 1 + head_devices - 1)

    place = core + PAIR * side
    t_copies = []
    for away in range(1, layer):
        peer = lax.rem(place + away, layer)
        t_copies.append(pltpu.make_async_remote_copy(
            src_ref=t_ref.at[place], dst_ref=t_ref.at[place],
            send_sem=t_send.at[away], recv_sem=t_recv.at[place],
            device_id={"seq": group + peer}, device_id_type=MESH,
        ))
        t_copies[-1].start()

    for head in range(heads):
        lanes = head_lanes(head)
        keys = k_ref[:, lanes].astype(F32) * column(2 * heads + head)
        upper, lower = halves(keys)
        value = v_ref[:, lanes]
        part_ref[0, head] = dot(upper, value, (0, 0)) + dot(lower, value, (0, 0))
        query = q_ref[:, lanes].astype(F32) * column(heads + head)
        upper, lower = halves(query)
        grad = g_ref[:, lanes]
        part_ref[1, head] = dot(upper, grad, (0, 0)) + dot(lower, grad, (0, 0))

    def mate_copy(way, j):
        return pltpu.make_async_remote_copy(
            src_ref=part_ref.at[way, (1 - core) * half + j], dst_ref=mate_ref.at[way, j],
            send_sem=mate_send.at[way, j], recv_sem=mate_recv.at[way, j],
            device_id={"seq": mate}, device_id_type=MESH,
        )

    for way in range(2):
        for j in range(half):
            mate_copy(way, j).start()

    for away in range(1, layer):
        source = lax.rem(place + layer - away, layer)
        pltpu.make_async_remote_copy(
            src_ref=t_ref.at[place], dst_ref=t_ref.at[source],
            send_sem=t_send.at[away], recv_sem=t_recv.at[source],
            device_id={"seq": group + source}, device_id_type=MESH,
        ).wait_recv()

    def decay_of(core_at, side_at, j):
        return t_ref[core_at + PAIR * side_at, pl.ds(core * half + j, 1), :]

    lower_mask = row_id >= col_id
    same_doc = lower_mask & (column(3 * heads) == doc_row)

    def local_head(head, sums):
        lanes = head_lanes(head)
        query, key, value, grad = q_ref[:, lanes], k_ref[:, lanes], v_ref[:, lanes], g_ref[:, lanes]
        spread = jnp.where(same_doc, column(head) - rows_ref[head:head + 1], 0.0)
        weights = jnp.where(same_doc, jnp.exp(spread), 0.0)
        scores = dot(query, key, (1, 1)) * scaling * weights
        pair_dots = dot(grad, value, (1, 1))
        weighted = (pair_dots * weights * scaling).astype(BF16)
        products = scores * pair_dots
        iv_ref[:, lanes] = dot(scores.astype(BF16), grad, (0, 0))
        iq_ref[:, lanes] = dot(weighted, key, (1, 0))
        ik_ref[:, lanes] = dot(weighted, query, (0, 0))
        sums.append(
            (jnp.sum(products, axis=1, keepdims=True), jnp.sum(products, axis=0, keepdims=True))
        )

    def chain_place(way):
        return jnp.where(way == 0, level, depth - 1 - level)

    def is_first(way, at):
        return jnp.where(way == 0, at, 1 - at) == 0

    def chain_copy(way, j):
        there = jnp.where(way == 0, level + 1, level - 1)
        return pltpu.make_async_remote_copy(
            src_ref=chain_out.at[way, j], dst_ref=chain_in.at[way, j],
            send_sem=chain_send.at[way, j], recv_sem=chain_recv.at[way, j],
            device_id={"seq": there * layer + side * PAIR + core}, device_id_type=MESH,
        )

    def side_copy(way, j):
        return pltpu.make_async_remote_copy(
            src_ref=side_out.at[way, j], dst_ref=side_in.at[way, j],
            send_sem=side_send.at[way, j], recv_sem=side_recv.at[way, j],
            device_id={"seq": across}, device_id_type=MESH,
        )

    def back_copy(way, j, owner):
        return pltpu.make_async_remote_copy(
            src_ref=back_out.at[way, j], dst_ref=state_ref.at[way, owner * half + j],
            send_sem=back_send.at[way, j], recv_sem=back_recv.at[way, j],
            device_id={"seq": mate}, device_id_type=MESH,
        )

    early = jnp.where(level * 2 < depth, 0, 1)

    def run_chain(way):
        here = chain_place(way)
        core_first = is_first(way, core)
        side_first = is_first(way, side)
        for j in range(half):
            mine, other = decay_of(core, side, j), decay_of(1 - core, side, j)
            chip = mine * other
            chip_other = decay_of(core, 1 - side, j) * decay_of(1 - core, 1 - side, j)
            mate_copy(way, j).wait_recv()
            agg_ref[way, j] = (
                jnp.where(core_first, other, 1.0) * part_ref[way, core * half + j]
                + jnp.where(core_first, 1.0, mine) * mate_ref[way, j]
            )

            @pl.when(here > 0)
            def _():
                chain_copy(way, j).wait_recv()

            @pl.when(here == 0)
            def _():
                chain_in[way, j] = jnp.zeros((HEAD_DIM, HEAD_DIM), F32)

            @pl.when(here < depth - 1)
            def _():
                chain_out[way, j] = (chip * chip_other) * chain_in[way, j] + jnp.where(
                    side_first, chip_other, 1.0
                ) * agg_ref[way, j]
                chain_copy(way, j).start()

            side_out[way, j] = jnp.where(side_first, chip, 1.0) * chain_in[way, j] + jnp.where(
                side_first, 1.0, 0.0
            ) * agg_ref[way, j]
            side_copy(way, j).start()

    def run_back(way):
        core_first = is_first(way, core)
        side_first = is_first(way, side)
        for j in range(half):
            mine, other = decay_of(core, side, j), decay_of(1 - core, side, j)
            chip_other = decay_of(core, 1 - side, j) * decay_of(1 - core, 1 - side, j)
            side_copy(way, j).wait_recv()
            entering = jnp.where(side_first, 1.0, chip_other) * chain_in[way, j] + side_in[way, j]
            back_out[way, j] = (
                jnp.where(core_first, mine, 1.0) * entering
                + jnp.where(core_first, 1.0, 0.0) * part_ref[way, core * half + j]
            )
            back_copy(way, j, core).start()
            state_ref[way, core * half + j] = (
                jnp.where(core_first, 1.0, other) * entering
                + jnp.where(core_first, 0.0, 1.0) * mate_ref[way, j]
            )

    sums = []
    run_chain(early)
    local_head(0, sums)
    if heads > 1:
        local_head(1, sums)
    run_chain(1 - early)
    for head in range(2, heads):
        local_head(head, sums)
    run_back(early)
    run_back(1 - early)
    for way in range(2):
        for j in range(half):
            back_copy(way, j, 1 - core).wait_recv()

    lane_id = lax.broadcasted_iota(jnp.int32, (rows, LANES), 1)
    gathered = jnp.zeros((rows, LANES), F32)
    ends = []
    for head in range(heads):
        lanes = head_lanes(head)
        query, key, value, grad = q_ref[:, lanes], k_ref[:, lanes], v_ref[:, lanes], g_ref[:, lanes]
        state, back = state_ref[0, head], state_ref[1, head]
        state_hi, state_lo = halves(state)
        back_hi, back_lo = halves(back)
        enter, leave = column(heads + head), column(2 * heads + head)
        grad_through = (dot(grad, state_hi, (1, 1)) + dot(grad, state_lo, (1, 1))) * enter
        key_carry = (dot(key, back_hi, (1, 0)) + dot(key, back_lo, (1, 0))) * leave
        value_carry = dot(value, back_hi, (1, 1)) * leave
        gq_ref[:, lanes] = (iq_ref[:, lanes] + grad_through).astype(BF16)
        gk_ref[:, lanes] = (ik_ref[:, lanes] + value_carry).astype(BF16)
        gv_ref[:, lanes] = (iv_ref[:, lanes] + key_carry).astype(BF16)
        inflow = jnp.sum(query.astype(F32) * grad_through, axis=1, keepdims=True)
        outflow = jnp.sum(value.astype(F32) * key_carry, axis=1, keepdims=True)
        whole = jnp.sum(jnp.sum(state * back, axis=0, keepdims=True), axis=1, keepdims=True)
        ends.append(
            through[head:head + 1] * whole + jnp.sum(outflow, axis=0, keepdims=True)
        )
        gathered = jnp.where(lane_id == head, sums[head][0] + inflow - outflow, gathered)
    turned = gathered.T[0:heads]
    across_sums = jnp.concatenate([s[1] for s in sums], axis=0)
    end_term = jnp.concatenate(ends, axis=0)
    row_lane = lax.broadcasted_iota(jnp.int32, (heads, rows), 1)
    grad_cumul = turned - across_sums + jnp.where(row_lane == rows - 1, end_term, 0.0)
    grad_log = dot(grad_cumul, (row_id >= col_id).astype(F32), (1, 0), precise)
    grad_gate = grad_log * (1.0 / (1.0 + jnp.exp(gate_rows))) / 16.0
    gw_part = dot(grad_gate, latent_ref[...].astype(F32), (1, 0), precise)
    gw_slots[flat, 0:heads, 0:gw_part.shape[1]] = gw_part
    lat_slots[my_head] = dot(weight_ref[...].astype(F32), grad_gate, (1, 0), precise)

    def lat_copy(away, slot, target):
        return pltpu.make_async_remote_copy(
            src_ref=lat_slots.at[slot], dst_ref=lat_slots.at[slot],
            send_sem=lat_send.at[away], recv_sem=lat_recv.at[slot],
            device_id={"head": target}, device_id_type=MESH,
        )

    def gw_copy(away, slot, target):
        return pltpu.make_async_remote_copy(
            src_ref=gw_slots.at[slot], dst_ref=gw_slots.at[slot],
            send_sem=gw_send.at[away], recv_sem=gw_recv.at[slot],
            device_id=member(target), device_id_type=MESH,
        )

    for away in range(1, members):
        gw_copy(away, flat, lax.rem(flat + away, members)).start()
    for away in range(1, head_devices):
        lat_copy(away, my_head, lax.rem(my_head + away, head_devices)).start()
    for away in range(1, head_devices):
        source = lax.rem(my_head + head_devices - away, head_devices)
        lat_copy(away, source, source).wait_recv()
    total = lat_slots[0]
    for slot in range(1, head_devices):
        total = total + lat_slots[slot]
    glat_ref[...] = total
    for away in range(1, members):
        source = lax.rem(flat + members - away, members)
        gw_copy(away, source, source).wait_recv()
    total = gw_slots[0]
    for slot in range(1, members):
        total = total + gw_slots[slot]
    gw_ref[...] = total

    for copy in t_copies:
        copy.wait_send()
    for way in range(2):
        for j in range(half):
            mate_copy(way, j).wait_send()
            side_copy(way, j).wait_send()
            back_copy(way, j, core).wait_send()

            @pl.when(chain_place(way) < depth - 1)
            def _():
                chain_copy(way, j).wait_send()
    for away in range(1, members):
        gw_copy(away, flat, lax.rem(flat + away, members)).wait_send()
    for away in range(1, head_devices):
        lat_copy(away, my_head, lax.rem(my_head + away, head_devices)).wait_send()


def on_device(sizes, *args):
    queries, keys_in, values, grad_out, latent, gate_weight, gate_bias, doc_starts, block_docs = args
    rows, width = queries.shape[1], queries.shape[2]
    rank = latent.shape[2]
    seq_count, dp_count, head_devices = sizes
    heads = width // HEAD_DIM
    half = heads // PAIR
    members = seq_count * dp_count
    depth = HEAD_DIM
    blocks = lambda *lead: pltpu.VMEM((*lead, depth, depth), F32)
    dma = lambda *shape: pltpu.SemaphoreType.DMA(shape)
    vmem = pl.BlockSpec(memory_space=pltpu.VMEM)
    wide = jax.ShapeDtypeStruct((rows, width), BF16)
    out = pl.pallas_call(
        functools.partial(kernel, (seq_count, dp_count, head_devices, heads)),
        out_shape=(
            wide, wide, wide,
            jax.ShapeDtypeStruct((rank, rows), F32),
            jax.ShapeDtypeStruct((8, LANES), F32),
        ),
        in_specs=[vmem] * 8,
        out_specs=(vmem,) * 5,
        scratch_shapes=[
            pltpu.VMEM((LANES, rows), F32),
            pltpu.VMEM((rows, LANES), F32),
            pltpu.VMEM((rows, width), F32),
            pltpu.VMEM((rows, width), F32),
            pltpu.VMEM((rows, width), F32),
            pltpu.VMEM((PAIR * SIDE, 8, LANES), F32),
            blocks(2, heads), blocks(2, half), blocks(2, half), blocks(2, half), blocks(2, half),
            blocks(2, half), blocks(2, half), blocks(2, half), blocks(2, heads),
            pltpu.VMEM((head_devices, rank, rows), F32),
            pltpu.VMEM((members, 8, LANES), F32),
            dma(PAIR * SIDE), dma(PAIR * SIDE),
            dma(2, half), dma(2, half), dma(2, half), dma(2, half), dma(2, half), dma(2, half),
            dma(2, half), dma(2, half),
            dma(head_devices), dma(head_devices),
            dma(members), dma(members),
        ],
        compiler_params=pltpu.CompilerParams(collective_id=0, has_side_effects=True),
        name="gated_backward",
    )(
        queries[0], keys_in[0], values[0], grad_out[0], latent[0], gate_weight,
        gate_bias[None, :], doc_starts,
    )
    return (
        out[0][None], out[1][None], out[2][None], out[3].T[None], out[4][0:heads, 0:rank].T,
    )


def solution(mesh):
    sizes = (mesh.shape["seq"], mesh.shape["dp"], mesh.shape["head"])
    return jax.shard_map(
        functools.partial(on_device, sizes),
        mesh=mesh,
        in_specs=(
            P(("groups", "dp"), "seq", "head"),
            P(("groups", "dp"), "seq", "head"),
            P(("groups", "dp"), "seq", "head"),
            P(("groups", "dp"), "seq", "head"),
            P(("groups", "dp"), "seq", None),
            P(None, "head"),
            P("head"),
            P(("groups", "dp"), None),
            P(("groups", "dp"), "seq"),
        ),
        out_specs=(
            P(("groups", "dp"), "seq", "head"),
            P(("groups", "dp"), "seq", "head"),
            P(("groups", "dp"), "seq", "head"),
            P(("groups", "dp"), "seq", None),
            P("groups", "head"),
        ),
        check_vma=False,
    )
```

profile of v0, /device:TPU:0, one launch (start us, length us, event | category | flops | bytes accessed | tf_op | source)
XLA Modules:
  0.0 40.2 jit_solution(806588696837778377)
XLA Ops:
  0.6 0.0 copy-start.3
  0.6 0.0 copy-start.4
  0.7 0.7 %copy-done.4 = bf16[16,4]{0,1:T(4,128)(2,1)S(1)} copy-done((bf16[16,4]{0,1:T(4,128)(2,1)S(1)}, bf16[16,4]{0,1:T(4,128)(2,1)}, u32[]{:S(2)}) %copy-start.4) | copy-done | bytes 152
  1.3 0.7 %copy.14.weight_ref = bf16[16,4]{1,0:T(8,128)(2,1)} copy(bf16[16,4]{0,1:T(4,128)(2,1)S(1)} %copy-done.4) | data formatting | bytes 256 | tf_op args[5]
  2.0 0.0 copy-done.3
  2.0 0.7 %copy.13 = bf16[1,256,16]{2,1,0:T(8,128)(2,1)} copy(bf16[1,256,16]{1,2,0:T(8,128)(2,1)S(1)} %copy-done.3) | data formatting | bytes 16384 | tf_op args[4]
  2.7 32.2 %gated_backward.1 = (bf16[256,512]{1,0:T(8,128)(2,1)}, bf16[256,512]{1,0:T(8,128)(2,1)}, bf16[256,512]{1,0:T(8,128)(2,1)}, f32[16,256]{1,0:T(8,128)}, f32[8,128]{1,0:T(8,128)}) custom-call(bf16[256,512]{1,0:T(8,128)(2,1)} %bitcast.14, bf16[256,512]{1,0:T(8,128)(2,1)} %bitcast.15, bf16[256,512]{1,0:T(8,128)(2,1)} %bitcast.16, bf16[256,512]{1,0:T(8,128)(2,1)} %bitcast.17, ...), custom_call_target="tpu_custom_call" | custom-call | tf_op jit(solution)/shard_map/gated_backward/pallas_call | solution.py:371
  34.9 0.0 copy-start.5
  34.9 0.7 %copy-done.5 = f32[8,128]{1,0:T(8,128)S(1)} copy-done((f32[8,128]{1,0:T(8,128)S(1)}, f32[8,128]{1,0:T(8,128)}, u32[]{:S(2)}) %copy-start.5) | copy-done | bytes 4120
  35.6 0.6 %slice_bitcast_fusion = f32[16,4]{0,1:T(4,128)} fusion(f32[8,128]{1,0:T(8,128)S(1)} %copy-done.5), kind=kLoop, calls=%fused_computation | loop fusion | bytes 512 | tf_op jit(solution)/shard_map/transpose | solution.py:404
  36.2 0.0 copy-start.1
  36.2 1.7 %copy.19 = bf16[1,256,512]{2,1,0:T(8,128)(2,1)} copy(bf16[1,256,512]{2,1,0:T(8,128)(2,1)} %bitcast.21) | data formatting | bytes 524288
  37.9 0.0 copy-done.1
  37.9 0.0 copy-start
  37.9 0.7 %copy.20 = bf16[1,256,512]{2,1,0:T(8,128)(2,1)} copy(bf16[1,256,512]{2,1,0:T(8,128)(2,1)S(1)} %bitcast.20) | data formatting | bytes 524288
  38.6 0.3 copy-done
  38.9 0.0 copy-start.2
  38.9 0.7 %copy.21 = bf16[1,256,512]{2,1,0:T(8,128)(2,1)} copy(bf16[1,256,512]{2,1,0:T(8,128)(2,1)S(1)} %bitcast.19) | data formatting | bytes 524288
  39.6 0.0 copy-done.2
  39.6 0.6 %copy.22 = f32[1,256,16]{1,2,0:T(8,128)} copy(f32[1,256,16]{1,2,0:T(8,128)S(1)} %bitcast.22) | data formatting | bytes 32768
Async XLA Ops:
  0.6 1.4 %copy-start.3 = (bf16[1,256,16]{1,2,0:T(8,128)(2,1)S(1)}, bf16[1,256,16]{1,2,0:T(8,128)(2,1)}, u32[]{:S(2)}) copy-start(bf16[1,256,16]{1,2,0:T(8,128)(2,1)} %param.13) | copy-start | bytes 24580
  0.6 0.7 %copy-start.4 = (bf16[16,4]{0,1:T(4,128)(2,1)S(1)}, bf16[16,4]{0,1:T(4,128)(2,1)}, u32[]{:S(2)}) copy-start(bf16[16,4]{0,1:T(4,128)(2,1)} %param.14) | copy-start | bytes 388
  34.9 0.7 %copy-start.5 = (f32[8,128]{1,0:T(8,128)S(1)}, f32[8,128]{1,0:T(8,128)}, u32[]{:S(2)}) copy-start(f32[8,128]{1,0:T(8,128)} %get-tuple-element.14) | copy-start | bytes 12292
  36.2 1.7 %copy-start.1 = (bf16[256,512]{1,0:T(8,128)(2,1)S(1)}, bf16[256,512]{1,0:T(8,128)(2,1)}, u32[]{:S(2)}) copy-start(bf16[256,512]{1,0:T(8,128)(2,1)} %get-tuple-element.11) | copy-start | bytes 786436
  37.9 1.0 %copy-start = (bf16[256,512]{1,0:T(8,128)(2,1)S(1)}, bf16[256,512]{1,0:T(8,128)(2,1)}, u32[]{:S(2)}) copy-start(bf16[256,512]{1,0:T(8,128)(2,1)} %get-tuple-element.12) | copy-start | bytes 786436
  38.9 0.7 %copy-start.2 = (f32[16,256]{1,0:T(8,128)S(1)}, f32[16,256]{1,0:T(8,128)}, u32[]{:S(2)}) copy-start(f32[16,256]{1,0:T(8,128)} %get-tuple-element.13) | copy-start | bytes 49156
where the time goes:
time: 40.6 us; the launch traced here: 40.2 us
  Pallas kernels  32.2 us (79%)
  local copies, waits for them, and re-layouts  7.42 us (18%)
  between operations  0.67 us (2%)
    pallas_call x1, Pallas kernels, on_device(): pl.pallas_call(functools.partial(kernel, (seq_count, dp_count, head_devic...  32.2 us
    unnamed x18, local copies, waits for them, and re-layouts  6.84 us

commit v1 on v0

--- a/solution.py
+++ b/solution.py
@@ -73,7 +73,7 @@
             device_id_type=MESH,
         )
 
-    gate_rows = dot(weight_ref[...], latent_ref[...], (0, 1))
+    gate_rows = dot(weight_ref[...], latent_ref[...], (1, 0))
     eye = lax.broadcasted_iota(jnp.int32, (heads, heads), 0) == lax.broadcasted_iota(
         jnp.int32, (heads, heads), 1
     )
@@ -301,9 +301,9 @@
     grad_cumul = turned - across_sums + jnp.where(row_lane == rows - 1, end_term, 0.0)
     grad_log = dot(grad_cumul, (row_id >= col_id).astype(F32), (1, 0), precise)
     grad_gate = grad_log * (1.0 / (1.0 + jnp.exp(gate_rows))) / 16.0
-    gw_part = dot(grad_gate, latent_ref[...].astype(F32), (1, 0), precise)
+    gw_part = dot(grad_gate, latent_ref[...].astype(F32), (1, 1), precise)
     gw_slots[flat, 0:heads, 0:gw_part.shape[1]] = gw_part
-    lat_slots[my_head] = dot(weight_ref[...].astype(F32), grad_gate, (1, 0), precise)
+    lat_slots[my_head] = dot(weight_ref[...].astype(F32), grad_gate, (0, 0), precise)
 
     def lat_copy(away, slot, target):
         return pltpu.make_async_remote_copy(
@@ -355,6 +355,31 @@
         lat_copy(away, my_head, lax.rem(my_head + away, head_devices)).wait_send()
 
 
+def final_kernel(gq, gk, gv, gl, gw, oq, ok, ov, ol, ow, sems):
+    copies = []
+    for i, (a, b) in enumerate(((gq, oq), (gk, ok), (gv, ov))):
+        copies.append(pltpu.make_async_copy(a, b, sems.at[i]))
+        copies[-1].start()
+    ol[...] = gl[...]
+    ow[...] = gw[0:ow.shape[0], 0:ow.shape[1]]
+    for c in copies:
+        c.wait()
+
+
+def emit(out, rows, width, rank, heads):
+    vm = pl.BlockSpec(memory_space=pltpu.VMEM)
+    any_ = pl.BlockSpec(memory_space=pl.ANY)
+    wide = jax.ShapeDtypeStruct((rows, width), BF16)
+    return pl.pallas_call(
+        final_kernel,
+        out_shape=(wide, wide, wide, jax.ShapeDtypeStruct((rank, rows), F32), jax.ShapeDtypeStruct((heads, rank), F32)),
+        in_specs=[vm] * 5,
+        out_specs=(any_, any_, any_, vm, vm),
+        scratch_shapes=[pltpu.SemaphoreType.DMA((3,))],
+        name="emit",
+    )(*(pltpu.with_memory_space_constraint(o, pltpu.VMEM) for o in out))
+
+
 def on_device(sizes, *args):
     queries, keys_in, values, grad_out, latent, gate_weight, gate_bias, doc_starts, block_docs = args
     rows, width = queries.shape[1], queries.shape[2]
@@ -371,12 +396,11 @@
     out = pl.pallas_call(
         functools.partial(kernel, (seq_count, dp_count, head_devices, heads)),
         out_shape=(
-            wide, wide, wide,
-            jax.ShapeDtypeStruct((rank, rows), F32),
-            jax.ShapeDtypeStruct((8, LANES), F32),
+            pltpu.VMEM((rows, width), BF16), pltpu.VMEM((rows, width), BF16), pltpu.VMEM((rows, width), BF16),
+            pltpu.VMEM((rank, rows), F32),
+            pltpu.VMEM((8, LANES), F32),
         ),
         in_specs=[vmem] * 8,
-        out_specs=(vmem,) * 5,
         scratch_shapes=[
             pltpu.VMEM((LANES, rows), F32),
             pltpu.VMEM((rows, LANES), F32),
@@ -397,11 +421,12 @@
         compiler_params=pltpu.CompilerParams(collective_id=0, has_side_effects=True),
         name="gated_backward",
     )(
-        queries[0], keys_in[0], values[0], grad_out[0], latent[0], gate_weight,
+        queries[0], keys_in[0], values[0], grad_out[0], latent[0].T, gate_weight.T,
         gate_bias[None, :], doc_starts,
     )
+    out = emit(out, rows, width, rank, heads)
     return (
-        out[0][None], out[1][None], out[2][None], out[3].T[None], out[4][0:heads, 0:rank].T,
+        out[0][None], out[1][None], out[2][None], out[3].T[None], out[4].T,
     )
 
 

time: 40.6 us -> 33.5 us (0.83)
  local copies, waits for them, and re-layouts: 7.42 us -> 0 us
  Pallas kernels: 32.2 us -> 32.7 us
    unnamed x18 -> x0, local copies, waits for them, and re-layouts: 6.84 us -> none
    pallas_call x0 -> x1, Pallas kernels: none -> 1.51 us  [emit(): pl.pallas_call(final_kernel, out_shape=(wide, wide, wide, jax.ShapeDtypeS...]
    pallas_call x1, Pallas kernels: 32.2 us -> 31.2 us  [on_device(): pl.pallas_call(functools.partial(kernel, (seq_count, dp_count, head_devic...]
    transpose x1 -> x0, local copies, waits for them, and re-layouts: 0.58 us -> none  [on_device(): out[4][0:heads, 0:rank]]
where the time goes in v1:
time: 33.5 us; the launch traced here: 33.4 us
  Pallas kernels  32.7 us (98%)
  between operations  0.64 us (2%)
    pallas_call x1, Pallas kernels, on_device(): pl.pallas_call(functools.partial(kernel, (seq_count, dp_count, head_devic...  31.2 us
    pallas_call x1, Pallas kernels, emit(): pl.pallas_call(final_kernel, out_shape=(wide, wide, wide, jax.ShapeDtypeS...  1.51 us

profile of v1, /device:TPU:0, one launch (start us, length us, event | category | flops | bytes accessed | tf_op | source)
XLA Modules:
  0.0 33.4 jit_solution(10920197334902606705)
XLA Ops:
  0.6 31.2 %gated_backward.1 = (bf16[256,512]{1,0:T(8,128)(2,1)S(1)}, bf16[256,512]{1,0:T(8,128)(2,1)S(1)}, bf16[256,512]{1,0:T(8,128)(2,1)S(1)}, f32[16,256]{1,0:T(8,128)S(1)}, f32[8,128]{1,0:T(8,128)S(1)}) custom-call(bf16[256,512]{1,0:T(8,128)(2,1)} %bitcast.16, bf16[256,512]{1,0:T(8,128)(2,1)} %bitcast.17, bf16[256,512]{1,0:T(8,128)(2,1)} %bitcast.18, ...), custom_call_target="tpu_custom_call" | custom-call | tf_op jit(solution)/shard_map/gated_backward/pallas_call | solution.py:396
  31.9 1.5 %emit.1 = (bf16[256,512]{1,0:T(8,128)(2,1)}, bf16[256,512]{1,0:T(8,128)(2,1)}, bf16[256,512]{1,0:T(8,128)(2,1)}, f32[16,256]{1,0:T(8,128)}, f32[4,16]{1,0:T(4,128)}) custom-call(bf16[256,512]{1,0:T(8,128)(2,1)S(1)} %get-tuple-element.15.gq, bf16[256,512]{1,0:T(8,128)(2,1)S(1)} %get-tuple-element.16.gk, bf16[256,512]{1,0:T(8,128)(2,1)S(1)} %get-tuple-element.17.gv, ...), custom_call_target="tpu_custom_call" | custom-call | tf_op jit(solution)/shard_map/emit/pallas_call | solution.py:373

commit v2 on v0

v2 whole, which is shorter than its diff:
```python
import functools
import math

import jax
import jax.numpy as jnp
from jax import lax
from jax.experimental import pallas as pl
from jax.experimental.pallas import tpu as pltpu
from jax.sharding import PartitionSpec as P

HEAD_DIM = 128
LANES = 128
PAIR = 2
CHIPS = 4
LEAD = 8
CHUNKS = 2
PIECE = HEAD_DIM // CHUNKS

MESH = pl.DeviceIdType.MESH
F32 = jnp.float32
BF16 = jnp.bfloat16


def dot(left, right, over):
    return lax.dot_general(
        left, right, (((over[0],), (over[1],)), ((), ())), preferred_element_type=F32,
    )


def halves(tensor):
    upper = tensor.astype(BF16)
    return upper, (tensor - upper.astype(F32)).astype(BF16)


def thirds(tensor):
    upper, rest = tensor.astype(BF16), None
    rest = tensor - upper.astype(F32)
    middle = rest.astype(BF16)
    return upper.astype(F32), middle.astype(F32), rest - middle.astype(F32)


def kernel(
    sizes,
    k_hbm, q_hbm, v_hbm, g_hbm, latent_hbm, weight_hbm, bias_hbm, bounds_hbm,
    gq_ref, gk_ref, gv_ref, glat_ref, gw_ref,
    x_ref, latent_ref, weight_ref, bias_ref, bounds_ref,
    stack_ref, rows_ref, cols_ref, upto_ref, iq_ref, ik_ref, iv_ref, flow_ref, down_ref,
    t_ref, part_ref, mate_in, rs_out, rs_in, blk_out, blk_in, ag_out, back_out, state_ref,
    lat_slots, gw_slots,
    load_sem, small_sem, t_send, t_recv, mate_send, mate_recv, rs_send, rs_recv,
    blk_send, blk_recv, ag_send, ag_recv, back_send, back_recv,
    lat_send, lat_recv, gw_send, gw_recv,
):
    seq_count, dp_count, head_devices, heads = sizes
    rows = x_ref.shape[1]
    quarter = heads // CHIPS
    layer = PAIR * CHIPS
    blocks = seq_count // layer
    pad = stack_ref.shape[0] // 3
    scaling = 1.0 / math.sqrt(HEAD_DIM)
    me = lax.axis_index("seq")
    my_dp = lax.axis_index("dp")
    my_head = lax.axis_index("head")
    core = lax.rem(me, PAIR)
    chip = lax.rem(lax.div(me, PAIR), CHIPS)
    block = lax.div(me, layer)
    group = block * layer
    place = core + PAIR * chip
    mate = me + 1 - 2 * core
    members = seq_count * dp_count
    flat = me * dp_count + my_dp
    beside = chip + 1 - 2 * lax.rem(chip, 2)
    above = chip + 2 - 4 * lax.div(chip, 2)
    opposite = CHIPS - 1 - chip
    others = (opposite, above, beside)

    def at_chip(index):
        return group + index * PAIR + core

    def at_block(distance):
        return me + jnp.where(core == 0, distance, -distance) * layer

    def sends_to(distance):
        return jnp.where(core == 0, block + distance < blocks, block >= distance)

    def hears_from(distance):
        return jnp.where(core == 0, block >= distance, block + distance < blocks)

    def member(index):
        return {"seq": lax.div(index, dp_count), "dp": lax.rem(index, dp_count)}

    small = [
        pltpu.make_async_copy(source, target, small_sem.at[index])
        for index, (source, target) in enumerate((
            (latent_hbm, latent_ref), (weight_hbm, weight_ref),
            (bias_hbm, bias_ref), (bounds_hbm, bounds_ref),
        ))
    ]
    loads = [
        pltpu.make_async_copy(source, x_ref.at[index], load_sem.at[index])
        for index, source in enumerate((k_hbm, q_hbm, v_hbm, g_hbm))
    ]
    for copy in small:
        copy.start()

    @pl.when(core == 0)
    def _():
        for index in (1, 3, 0, 2):
            loads[index].start()

    @pl.when(core == 1)
    def _():
        for index in (0, 2, 1, 3):
            loads[index].start()

    barrier = pltpu.get_barrier_semaphore()
    for away in range(1, members):
        pl.semaphore_signal(
            barrier, inc=1, device_id=member(lax.rem(flat + away, members)), device_id_type=MESH
        )
    for away in range(1, head_devices):
        pl.semaphore_signal(
            barrier, inc=1, device_id={"head": lax.rem(my_head + away, head_devices)},
            device_id_type=MESH,
        )

    row_id = lax.broadcasted_iota(jnp.int32, (rows, rows), 0)
    col_id = lax.broadcasted_iota(jnp.int32, (rows, rows), 1)
    upto_ref[...] = (row_id <= col_id).astype(F32).astype(BF16)
    stack_ref[...] = jnp.zeros_like(stack_ref)
    rows_ref[...] = jnp.zeros_like(rows_ref)
    flow_ref[...] = jnp.zeros_like(flow_ref)

    def stacked(tensor):
        for index, piece in enumerate(thirds(tensor)):
            stack_ref[index * pad:index * pad + heads] = piece
        return stack_ref[...].astype(BF16)

    def unstacked(tensor):
        return (tensor[0:heads] + tensor[pad:pad + heads]) + tensor[2 * pad:2 * pad + heads]

    for copy in small:
        copy.wait()
    gate_rows = dot(weight_ref[...], latent_ref[...], (1, 0))
    eye = lax.broadcasted_iota(jnp.int32, (heads, heads), 0) == lax.broadcasted_iota(
        jnp.int32, (heads, heads), 1
    )
    bias = jnp.sum(jnp.where(eye, bias_ref[...], 0.0), axis=1, keepdims=True)
    gate_rows = gate_rows + bias
    log_decay = (jnp.minimum(gate_rows, 0.0) - jnp.log1p(jnp.exp(-jnp.abs(gate_rows)))) / 16.0
    cumul = unstacked(dot(stacked(log_decay), upto_ref[...], (1, 0)))
    first_pos = me * rows
    bounds = bounds_ref[...]
    position = first_pos + lax.broadcasted_iota(jnp.int32, (rows, bounds.shape[1]), 0)
    opened = jnp.where((bounds >= first_pos) & (bounds <= position), 1.0, 0.0).astype(BF16)
    docs = dot(jnp.ones((8, bounds.shape[1]), BF16), opened, (1, 1))
    doc_row = docs[0:1]
    doc_last = doc_row[:, rows - 1:]
    ending = cumul[:, rows - 1:]
    through = jnp.where(doc_last == 0.0, jnp.exp(ending), 0.0)
    rows_ref[0:heads] = jnp.where(doc_row == doc_last, jnp.exp(ending - cumul), 0.0)
    rows_ref[heads:2 * heads] = jnp.where(doc_row == 0.0, jnp.exp(cumul), 0.0) * scaling
    rows_ref[2 * heads:3 * heads] = cumul
    rows_ref[3 * heads:3 * heads + 8] = docs
    t_ref[place, 0:heads] = jnp.broadcast_to(through, (heads, LANES))

    def column(index):
        return cols_ref[:, index:index + 1]

    def head_lanes(index):
        return pl.ds(index * HEAD_DIM, HEAD_DIM)

    def remote(source, target, send_sem, recv_sem, **where):
        return pltpu.make_async_remote_copy(
            src_ref=source, dst_ref=target, send_sem=send_sem, recv_sem=recv_sem,
            device_id=where, device_id_type=MESH,
        )

    pl.semaphore_wait(barrier, members - 1 + head_devices - 1)

    for away in range(1, layer):
        remote(
            t_ref.at[place], t_ref.at[place], t_send, t_recv,
            seq=group + lax.rem(place + away, layer),
        ).start()

    def mate_copy(head):
        return remote(
            part_ref.at[1 - core, head], mate_in.at[head], mate_send, mate_recv.at[head], seq=mate
        )

    def span(c):
        return pl.ds(c * PIECE, PIECE)

    def block_span(c):
        return pl.ds(0, LEAD + PIECE) if c == 0 else pl.ds(LEAD + c * PIECE, PIECE)

    def rs_copy(target, source, i, c):
        return remote(
            rs_out.at[target, i, span(c)], rs_in.at[source, i, span(c)],
            rs_send, rs_recv.at[source, c], seq=at_chip(target),
        )

    def blk_copy(distance, i, c):
        return remote(
            blk_out.at[i, block_span(c)], blk_in.at[distance - 1, i, block_span(c)],
            blk_send.at[distance - 1], blk_recv.at[distance - 1, c], seq=at_block(distance),
        )

    def ag_copy(target, source, i, c):
        return remote(
            ag_out.at[target, i, span(c)], state_ref.at[core, source * quarter + i, span(c)],
            ag_send, ag_recv.at[source, c], seq=at_chip(target),
        )

    def back_copy(head):
        return remote(
            back_out.at[head], state_ref.at[core, head], back_send, back_recv, seq=mate
        )

    order = [(whose, i) for whose in (*others, chip) for i in range(quarter)]

    def part(way, head):
        lanes = pl.ds(pl.multiple_of(head * HEAD_DIM, HEAD_DIM), HEAD_DIM)
        turned = x_ref[way, :, lanes].astype(F32).T
        upper, lower = halves(turned * rows_ref[pl.ds(way * heads + head, 1)])
        right = x_ref[2 + way, :, lanes]
        part_ref[way, head] = dot(upper, right, (1, 0)) + dot(lower, right, (1, 0))

    def load_wait(way):
        for index in (way, 2 + way):
            pltpu.make_async_copy(k_hbm, x_ref.at[index], load_sem.at[index]).wait()

    load_wait(1 - core)
    for whose, i in order:
        head = whose * quarter + i
        part(1 - core, head)
        mate_copy(head).start()
    load_wait(core)
    for whose, i in order:
        part(core, whose * quarter + i)

    passed = t_ref.at[pl.ds(0, layer - 1)]
    remote(passed, passed, t_send, t_recv, seq=mate).wait_recv()

    def decay_of(index, head):
        return t_ref[index, pl.ds(head, 1), :]

    for whose, i in order:
        head = whose * quarter + i
        keep = decay_of(PAIR * chip + 1 - core, head)
        mate_copy(head).wait_recv()
        for c in range(CHUNKS):
            total = keep * part_ref[core, head, span(c)] + mate_in[head, span(c)]
            if whose is chip:
                rs_in[chip, i, span(c)] = total
            else:
                rs_out[whose, i, span(c)] = total
                rs_copy(whose, chip, i, c).start()

    lane_id = lax.broadcasted_iota(jnp.int32, (rows, LANES), 1)

    def local_head(head):
        lanes = head_lanes(head)
        key, query, value, grad = (x_ref[index, :, lanes] for index in range(4))
        same_doc = (row_id >= col_id) & (column(3 * heads) == rows_ref[3 * heads:3 * heads + 1])
        spread = jnp.where(
            same_doc, column(2 * heads + head) - rows_ref[2 * heads + head:2 * heads + head + 1], 0.0
        )
        weights = jnp.where(same_doc, jnp.exp(spread), 0.0)
        scores = dot(query, key, (1, 1)) * scaling * weights
        pair_dots = dot(grad, value, (1, 1))
        weighted = (pair_dots * weights * scaling).astype(BF16)
        products = scores * pair_dots
        iv_ref[:, lanes] = dot(scores.astype(BF16), grad, (0, 0))
        iq_ref[:, lanes] = dot(weighted, key, (1, 0))
        ik_ref[:, lanes] = dot(weighted, query, (0, 0))
        flow_ref[...] += jnp.where(
            lane_id == head, jnp.sum(products, axis=1, keepdims=True), 0.0
        )
        down_ref[head:head + 1] = jnp.sum(products, axis=0, keepdims=True)

    cols_ref[...] = rows_ref[...].T
    for head in range(heads):
        local_head(head)

    def kth(k):
        return jnp.where(core == 0, k, CHIPS - 1 - k)

    def chip_decay(index, head):
        return decay_of(PAIR * index, head) * decay_of(PAIR * index + 1, head)

    for c in range(CHUNKS):
        for i in range(quarter):
            for source in others:
                rs_copy(source, source, i, c).wait_recv()
            head = chip * quarter + i
            total = rs_in[kth(0), i, span(c)]
            for k in range(1, CHIPS):
                total = chip_decay(kth(k), head) * total + rs_in[kth(k), i, span(c)]
            blk_out[i, pl.ds(LEAD + c * PIECE, PIECE)] = total
            if c == 0:
                across = chip_decay(0, head)
                for k in range(1, CHIPS):
                    across = across * chip_decay(k, head)
                blk_out[i, 0:LEAD] = jnp.broadcast_to(across, (LEAD, LANES))
            for distance in range(1, blocks):
                pl.when(sends_to(distance))(blk_copy(distance, i, c).start)

    for c in range(CHUNKS):
        for i in range(quarter):
            entering = jnp.zeros((PIECE, HEAD_DIM), F32)
            for distance in range(blocks - 1, 0, -1):
                hears = hears_from(distance)
                pl.when(hears)(blk_copy(distance, i, c).wait_recv)

                @pl.when(jnp.logical_not(hears))
                def _():
                    blk_in[distance - 1, i, block_span(c)] = jnp.zeros(
                        (PIECE + (LEAD if c == 0 else 0), HEAD_DIM), F32
                    )

                entering = (
                    blk_in[distance - 1, i, 0:1] * entering
                    + blk_in[distance - 1, i, pl.ds(LEAD + c * PIECE, PIECE)]
                )
            head = chip * quarter + i
            for k in range(CHIPS):
                ag_out[kth(k), i, span(c)] = entering
                if k < CHIPS - 1:
                    entering = chip_decay(kth(k), head) * entering + rs_in[kth(k), i, span(c)]
            for target in others:
                ag_copy(target, chip, i, c).start()

    for whose, i in ((whose, i) for whose in (chip, beside, above, opposite) for i in range(quarter)):
        head = whose * quarter + i
        if whose is chip:
            state_ref[core, head] = ag_out[chip, i]
        else:
            for c in range(CHUNKS):
                ag_copy(whose, whose, i, c).wait_recv()
        back_out[head] = decay_of(place, head) * state_ref[core, head] + part_ref[core, head]
        back_copy(head).start()

    def finish_state():
        for head in range(heads):
            lanes = head_lanes(head)
            query, grad = x_ref[1, :, lanes], x_ref[3, :, lanes]
            upper, lower = halves(state_ref[0, head])
            carried = (dot(grad, upper, (1, 1)) + dot(grad, lower, (1, 1))) * column(heads + head)
            gq_ref[:, lanes] = (iq_ref[:, lanes] + carried).astype(BF16)
            inflow = jnp.sum(query.astype(F32) * carried, axis=1, keepdims=True)
            flow_ref[...] += jnp.where(lane_id == head, inflow, 0.0)

    def finish_back():
        for head in range(heads):
            lanes = head_lanes(head)
            key, value = x_ref[0, :, lanes], x_ref[2, :, lanes]
            upper, lower = halves(state_ref[1, head])
            leave = column(head)
            carried = (dot(key, upper, (1, 0)) + dot(key, lower, (1, 0))) * leave
            gv_ref[:, lanes] = (iv_ref[:, lanes] + carried).astype(BF16)
            outflow = jnp.sum(value.astype(F32) * carried, axis=1, keepdims=True)
            flow_ref[...] -= jnp.where(lane_id == head, outflow, 0.0)
            total = jnp.sum(outflow, axis=0, keepdims=True)
            down_ref[heads + head:heads + head + 1] = jnp.broadcast_to(total, (1, rows))
            gk_ref[:, lanes] = (
                ik_ref[:, lanes] + dot(value, upper, (1, 1)) * leave
            ).astype(BF16)

    pl.when(core == 0)(finish_state)
    pl.when(core == 1)(finish_back)
    remote(back_out, state_ref.at[1 - core], back_send, back_recv, seq=mate).wait_recv()
    pl.when(core == 0)(finish_back)
    pl.when(core == 1)(finish_state)

    turned = flow_ref[...].T[0:heads]
    wholes = [
        jnp.sum(jnp.sum(state_ref[0, head] * state_ref[1, head], axis=0, keepdims=True), axis=1, keepdims=True)
        for head in range(heads)
    ]
    end_term = through * jnp.concatenate(wholes, axis=0) + down_ref[heads:2 * heads]
    row_lane = lax.broadcasted_iota(jnp.int32, (heads, rows), 1)
    grad_cumul = turned - down_ref[0:heads] + jnp.where(row_lane == rows - 1, end_term, 0.0)
    grad_log = unstacked(dot(stacked(grad_cumul), upto_ref[...], (1, 1)))
    grad_gate = grad_log * (1.0 / (1.0 + jnp.exp(gate_rows))) / 16.0
    pieces = stacked(grad_gate)
    gw_part = unstacked(dot(pieces, latent_ref[...], (1, 1)))
    gw_slots[flat, 0:heads, 0:gw_part.shape[1]] = gw_part
    weight = weight_ref[...]
    lat_slots[my_head] = (
        dot(weight, pieces[0:heads], (0, 0)) + dot(weight, pieces[pad:pad + heads], (0, 0))
    ) + dot(weight, pieces[2 * pad:2 * pad + heads], (0, 0))

    for away in range(1, members):
        remote(
            gw_slots.at[flat], gw_slots.at[flat], gw_send, gw_recv,
            **member(lax.rem(flat + away, members)),
        ).start()
    for away in range(1, head_devices):
        remote(
            lat_slots.at[my_head], lat_slots.at[my_head], lat_send, lat_recv,
            head=lax.rem(my_head + away, head_devices),
        ).start()

    peer = {"head": lax.rem(my_head + 1, head_devices)}
    if head_devices > 1:
        passed = lat_slots.at[pl.ds(0, head_devices - 1)]
        lats = remote(passed, passed, lat_send, lat_recv, **peer)
        lats.wait_recv()
    total = lat_slots[0]
    for slot in range(1, head_devices):
        total = total + lat_slots[slot]
    glat_ref[...] = total
    passed = gw_slots.at[pl.ds(0, members - 1)]
    sums = remote(passed, passed, gw_send, gw_recv, seq=mate)
    sums.wait_recv()
    total = gw_slots[0]
    for slot in range(1, members):
        total = total + gw_slots[slot]
    gw_ref[...] = total

    passed = t_ref.at[pl.ds(0, layer - 1)]
    remote(passed, passed, t_send, t_recv, seq=mate).wait_send()
    remote(mate_in, mate_in, mate_send, mate_recv.at[0], seq=mate).wait_send()
    passed = rs_out.at[pl.ds(0, CHIPS - 1)]
    remote(passed, passed, rs_send, rs_recv.at[0, 0], seq=mate).wait_send()
    passed = ag_out.at[pl.ds(0, CHIPS - 1)]
    remote(passed, passed, ag_send, ag_recv.at[0, 0], seq=mate).wait_send()
    remote(back_out, back_out, back_send, back_recv, seq=mate).wait_send()
    for distance in range(1, blocks):
        pl.when(sends_to(distance))(
            remote(
                blk_out, blk_out, blk_send.at[distance - 1], blk_recv.at[0, 0], seq=mate
            ).wait_send
        )
    if head_devices > 1:
        lats.wait_send()
    sums.wait_send()


def emit_kernel(gq, gk, gv, glat, gw, oq, ok, ov, olat, ow, sems):
    copies = [
        pltpu.make_async_copy(source, target, sems.at[index])
        for index, (source, target) in enumerate(((gq, oq), (gk, ok), (gv, ov)))
    ]
    for copy in copies:
        copy.start()
    olat[...] = glat[...]
    ow[...] = gw[0:ow.shape[0], 0:ow.shape[1]]
    for copy in copies:
        copy.wait()


def emit(results, rows, width, rank, heads):
    vmem = pl.BlockSpec(memory_space=pltpu.VMEM)
    hbm = pl.BlockSpec(memory_space=pl.ANY)
    wide = jax.ShapeDtypeStruct((rows, width), BF16)
    return pl.pallas_call(
        emit_kernel,
        out_shape=(
            wide, wide, wide,
            jax.ShapeDtypeStruct((rank, rows), F32), jax.ShapeDtypeStruct((heads, rank), F32),
        ),
        in_specs=[vmem] * 5,
        out_specs=(hbm, hbm, hbm, vmem, vmem),
        scratch_shapes=[pltpu.SemaphoreType.DMA((3,))],
        name="emit",
    )(*(pltpu.with_memory_space_constraint(result, pltpu.VMEM) for result in results))


def on_device(sizes, *args):
    queries, keys_in, values, grad_out, latent, gate_weight, gate_bias, doc_starts, block_docs = args
    rows, width = queries.shape[1], queries.shape[2]
    rank = latent.shape[2]
    seq_count, dp_count, head_devices = sizes
    heads = width // HEAD_DIM
    quarter = heads // CHIPS
    layer = PAIR * CHIPS
    far = max(1, seq_count // layer - 1)
    members = seq_count * dp_count
    pad = -(-heads // 8) * 8
    square = lambda *lead: pltpu.VMEM((*lead, HEAD_DIM, HEAD_DIM), F32)
    dma = lambda *shape: pltpu.SemaphoreType.DMA(shape)
    single = pltpu.SemaphoreType.DMA
    hbm = pl.BlockSpec(memory_space=pltpu.HBM)
    wide = pltpu.VMEM((rows, width), BF16)
    results = pl.pallas_call(
        functools.partial(kernel, (seq_count, dp_count, head_devices, heads)),
        out_shape=(
            wide, wide, wide, pltpu.VMEM((rank, rows), F32), pltpu.VMEM((8, LANES), F32),
        ),
        in_specs=[hbm] * 8,
        scratch_shapes=[
            pltpu.VMEM((4, rows, width), BF16),
            pltpu.VMEM((rank, rows), BF16),
            pltpu.VMEM((heads, rank), BF16),
            pltpu.VMEM((1, heads), F32),
            pltpu.VMEM(doc_starts.shape, jnp.int32),
            pltpu.VMEM((3 * pad, rows), F32),
            pltpu.VMEM((LANES, rows), F32),
            pltpu.VMEM((rows, LANES), F32),
            pltpu.VMEM((rows, rows), BF16),
            pltpu.VMEM((rows, width), F32),
            pltpu.VMEM((rows, width), F32),
            pltpu.VMEM((rows, width), F32),
            pltpu.VMEM((rows, LANES), F32),
            pltpu.VMEM((2 * pad, rows), F32),
            pltpu.VMEM((layer, 8, LANES), F32),
            square(2, heads), square(heads), square(CHIPS, quarter), square(CHIPS, quarter),
            pltpu.VMEM((quarter, LEAD + HEAD_DIM, HEAD_DIM), F32),
            pltpu.VMEM((far, quarter, LEAD + HEAD_DIM, HEAD_DIM), F32),
            square(CHIPS, quarter), square(heads), square(2, heads),
            pltpu.VMEM((head_devices, rank, rows), F32),
            pltpu.VMEM((members, 8, LANES), F32),
            dma(4), dma(4), single, single, single, dma(heads), single, dma(CHIPS, CHUNKS),
            dma(far), dma(far, CHUNKS), single, dma(CHIPS, CHUNKS), single, single,
            single, single, single, single,
        ],
        compiler_params=pltpu.CompilerParams(collective_id=0, has_side_effects=True),
        name="gated_backward",
    )(
        keys_in[0], queries[0], values[0], grad_out[0], latent[0].T, gate_weight.T,
        gate_bias[None, :], doc_starts,
    )
    out = emit(results, rows, width, rank, heads)
    return out[0][None], out[1][None], out[2][None], out[3].T[None], out[4].T


def solution(mesh):
    sizes = (mesh.shape["seq"], mesh.shape["dp"], mesh.shape["head"])
    return jax.shard_map(
        functools.partial(on_device, sizes),
        mesh=mesh,
        in_specs=(
            P(("groups", "dp"), "seq", "head"),
            P(("groups", "dp"), "seq", "head"),
            P(("groups", "dp"), "seq", "head"),
            P(("groups", "dp"), "seq", "head"),
            P(("groups", "dp"), "seq", None),
            P(None, "head"),
            P("head"),
            P(("groups", "dp"), None),
            P(("groups", "dp"), "seq"),
        ),
        out_specs=(
            P(("groups", "dp"), "seq", "head"),
            P(("groups", "dp"), "seq", "head"),
            P(("groups", "dp"), "seq", "head"),
            P(("groups", "dp"), "seq", None),
            P("groups", "head"),
        ),
        check_vma=False,
    )
```

time: 40.6 us -> 29.9 us (0.74)
  local copies, waits for them, and re-layouts: 7.42 us -> 0 us
  Pallas kernels: 32.2 us -> 29 us
    unnamed x18 -> x0, local copies, waits for them, and re-layouts: 6.84 us -> none
    pallas_call x1, Pallas kernels: 32.2 us -> 27.5 us  [on_device(): pl.pallas_call(functools.partial(kernel, (seq_count, dp_count, head_devic...]
    pallas_call x0 -> x1, Pallas kernels: none -> 1.51 us  [emit(): pl.pallas_call(emit_kernel, out_shape=(wide, wide, wide, jax.ShapeDtypeSt...]
    transpose x1 -> x0, local copies, waits for them, and re-layouts: 0.58 us -> none  [on_device(): out[4][0:heads, 0:rank]]
where the time goes in v2:
time: 29.9 us; the launch traced here: 29.7 us
  Pallas kernels  29 us (97%)
  between operations  0.64 us (2%)
    pallas_call x1, Pallas kernels, on_device(): pl.pallas_call(functools.partial(kernel, (seq_count, dp_count, head_devic...  27.5 us
    pallas_call x1, Pallas kernels, emit(): pl.pallas_call(emit_kernel, out_shape=(wide, wide, wide, jax.ShapeDtypeSt...  1.51 us

profile of v2, /device:TPU:0, one launch (start us, length us, event | category | flops | bytes accessed | tf_op | source)
XLA Modules:
  0.0 29.7 jit_solution(3725052732621200979)
XLA Ops:
  0.6 27.5 %gated_backward.1 = (bf16[256,512]{1,0:T(8,128)(2,1)S(1)}, bf16[256,512]{1,0:T(8,128)(2,1)S(1)}, bf16[256,512]{1,0:T(8,128)(2,1)S(1)}, f32[16,256]{1,0:T(8,128)S(1)}, f32[8,128]{1,0:T(8,128)S(1)}) custom-call(bf16[256,512]{1,0:T(8,128)(2,1)} %bitcast.16, bf16[256,512]{1,0:T(8,128)(2,1)} %bitcast.17, bf16[256,512]{1,0:T(8,128)(2,1)} %bitcast.18, ...), custom_call_target="tpu_custom_call" | custom-call | tf_op jit(solution)/shard_map/gated_backward/pallas_call | solution.py:488
  28.2 1.5 %emit.1 = (bf16[256,512]{1,0:T(8,128)(2,1)}, bf16[256,512]{1,0:T(8,128)(2,1)}, bf16[256,512]{1,0:T(8,128)(2,1)}, f32[16,256]{1,0:T(8,128)}, f32[4,16]{1,0:T(4,128)}) custom-call(bf16[256,512]{1,0:T(8,128)(2,1)S(1)} %get-tuple-element.15.gq, bf16[256,512]{1,0:T(8,128)(2,1)S(1)} %get-tuple-element.16.gk, bf16[256,512]{1,0:T(8,128)(2,1)S(1)} %get-tuple-element.17.gv, ...), custom_call_target="tpu_custom_call" | custom-call | tf_op jit(solution)/shard_map/emit/pallas_call | solution.py:459

commit v3 on v2

--- a/solution.py
+++ b/solution.py
@@ -13,7 +13,7 @@
 PAIR = 2
 CHIPS = 4
 LEAD = 8
-CHUNKS = 2
+CHUNKS = 4
 PIECE = HEAD_DIM // CHUNKS
 
 MESH = pl.DeviceIdType.MESH
@@ -44,18 +44,19 @@
     k_hbm, q_hbm, v_hbm, g_hbm, latent_hbm, weight_hbm, bias_hbm, bounds_hbm,
     gq_ref, gk_ref, gv_ref, glat_ref, gw_ref,
     x_ref, latent_ref, weight_ref, bias_ref, bounds_ref,
-    stack_ref, rows_ref, cols_ref, upto_ref, iq_ref, ik_ref, iv_ref, flow_ref, down_ref,
+    tiled_ref, stack_ref, rows_ref, cols_ref, upto_ref, iq_ref, ik_ref, iv_ref, flow_ref, down_ref,
     t_ref, part_ref, mate_in, rs_out, rs_in, blk_out, blk_in, ag_out, back_out, state_ref,
     lat_slots, gw_slots,
     load_sem, small_sem, t_send, t_recv, mate_send, mate_recv, rs_send, rs_recv,
     blk_send, blk_recv, ag_send, ag_recv, back_send, back_recv,
-    lat_send, lat_recv, gw_send, gw_recv,
+    lat_send, lat_recv, gw_send, gw_recv, block_ready, head_ready,
 ):
     seq_count, dp_count, head_devices, heads = sizes
     rows = x_ref.shape[1]
     quarter = heads // CHIPS
     layer = PAIR * CHIPS
     blocks = seq_count // layer
+    rank = latent_ref.shape[0]
     pad = stack_ref.shape[0] // 3
     scaling = 1.0 / math.sqrt(HEAD_DIM)
     me = lax.axis_index("seq")
@@ -89,6 +90,9 @@
     def member(index):
         return {"seq": lax.div(index, dp_count), "dp": lax.rem(index, dp_count)}
 
+    def greet(semaphore, **where):
+        pl.semaphore_signal(semaphore, inc=1, device_id=where, device_id_type=MESH)
+
     small = [
         pltpu.make_async_copy(source, target, small_sem.at[index])
         for index, (source, target) in enumerate((
@@ -114,15 +118,26 @@
             loads[index].start()
 
     barrier = pltpu.get_barrier_semaphore()
-    for away in range(1, members):
-        pl.semaphore_signal(
-            barrier, inc=1, device_id=member(lax.rem(flat + away, members)), device_id_type=MESH
-        )
-    for away in range(1, head_devices):
-        pl.semaphore_signal(
-            barrier, inc=1, device_id={"head": lax.rem(my_head + away, head_devices)},
-            device_id_type=MESH,
-        )
+    greeted = layer - 1 + seq_count * (dp_count - 1)
+    for away in range(1, layer):
+        greet(barrier, seq=group + lax.rem(place + away, layer))
+    for away in range(1, dp_count):
+        for there in range(seq_count):
+            greet(barrier, seq=there, dp=lax.rem(my_dp + away, dp_count))
+    for distance in range(1, blocks):
+
+        @pl.when(block + distance < blocks)
+        def _():
+            greet(barrier, seq=me + distance * layer)
+
+        greeted = greeted + jnp.where(block >= distance, 1, 0)
+    for distance in range(1, head_devices):
+
+        @pl.when(my_head + distance < head_devices)
+        def _():
+            greet(barrier, head=my_head + distance)
+
+        greeted = greeted + jnp.where(my_head >= distance, 1, 0)
 
     row_id = lax.broadcasted_iota(jnp.int32, (rows, rows), 0)
     col_id = lax.broadcasted_iota(jnp.int32, (rows, rows), 1)
@@ -176,13 +191,30 @@
             device_id=where, device_id_type=MESH,
         )
 
-    pl.semaphore_wait(barrier, members - 1 + head_devices - 1)
-
-    for away in range(1, layer):
-        remote(
-            t_ref.at[place], t_ref.at[place], t_send, t_recv,
-            seq=group + lax.rem(place + away, layer),
-        ).start()
+    pl.semaphore_wait(barrier, greeted)
+    for distance in range(1, blocks):
+
+        @pl.when(block >= distance)
+        def _():
+            greet(block_ready.at[distance - 1], seq=me - distance * layer)
+
+    for distance in range(1, head_devices):
+
+        @pl.when(my_head >= distance)
+        def _():
+            greet(head_ready.at[distance - 1], head=my_head - distance)
+
+
+    def decay_copy(target, slot):
+        return remote(
+            t_ref.at[slot], t_ref.at[slot], t_send,
+            t_recv.at[0 if target is mate else 1], seq=target,
+        )
+
+    decay_copy(mate, place).start()
+    for whose in others:
+        for peer in range(PAIR):
+            decay_copy(group + whose * PAIR + peer, place).start()
 
     def mate_copy(head):
         return remote(
@@ -240,8 +272,7 @@
     for whose, i in order:
         part(core, whose * quarter + i)
 
-    passed = t_ref.at[pl.ds(0, layer - 1)]
-    remote(passed, passed, t_send, t_recv, seq=mate).wait_recv()
+    decay_copy(mate, place).wait_recv()
 
     def decay_of(index, head):
         return t_ref[index, pl.ds(head, 1), :]
@@ -280,6 +311,8 @@
         )
         down_ref[head:head + 1] = jnp.sum(products, axis=0, keepdims=True)
 
+    for index in range(LANES // rank):
+        tiled_ref[index * rank:(index + 1) * rank] = latent_ref[...]
     cols_ref[...] = rows_ref[...].T
     for head in range(heads):
         local_head(head)
@@ -289,6 +322,14 @@
 
     def chip_decay(index, head):
         return decay_of(PAIR * index, head) * decay_of(PAIR * index + 1, head)
+
+    passed = t_ref.at[pl.ds(0, layer - PAIR)]
+    remote(passed, passed, t_send, t_recv.at[1], seq=mate).wait_recv()
+    for distance in range(1, blocks):
+
+        @pl.when(block + distance < blocks)
+        def _():
+            pl.semaphore_wait(block_ready.at[distance - 1], 1)
 
     for c in range(CHUNKS):
         for i in range(quarter):
@@ -364,9 +405,12 @@
             flow_ref[...] -= jnp.where(lane_id == head, outflow, 0.0)
             total = jnp.sum(outflow, axis=0, keepdims=True)
             down_ref[heads + head:heads + head + 1] = jnp.broadcast_to(total, (1, rows))
-            gk_ref[:, lanes] = (
-                ik_ref[:, lanes] + dot(value, upper, (1, 1)) * leave
-            ).astype(BF16)
+
+    def finish_keys():
+        for head in range(heads):
+            lanes = head_lanes(head)
+            carried = dot(x_ref[2, :, lanes], state_ref[1, head].astype(BF16), (1, 1)) * column(head)
+            gk_ref[:, lanes] = (ik_ref[:, lanes] + carried).astype(BF16)
 
     pl.when(core == 0)(finish_state)
     pl.when(core == 1)(finish_back)
@@ -385,12 +429,22 @@
     grad_log = unstacked(dot(stacked(grad_cumul), upto_ref[...], (1, 1)))
     grad_gate = grad_log * (1.0 / (1.0 + jnp.exp(gate_rows))) / 16.0
     pieces = stacked(grad_gate)
-    gw_part = unstacked(dot(pieces, latent_ref[...], (1, 1)))
-    gw_slots[flat, 0:heads, 0:gw_part.shape[1]] = gw_part
+    spread = unstacked(dot(pieces, tiled_ref[...], (1, 1)))
+    lane = lax.broadcasted_iota(jnp.int32, (heads, LANES), 1)
+    owner = lax.broadcasted_iota(jnp.int32, (heads, LANES), 0)
+    gw_slots[flat] = jnp.sum(
+        jnp.where(lax.div(lane, rank) == owner, spread, 0.0), axis=0, keepdims=True
+    )
     weight = weight_ref[...]
     lat_slots[my_head] = (
         dot(weight, pieces[0:heads], (0, 0)) + dot(weight, pieces[pad:pad + heads], (0, 0))
     ) + dot(weight, pieces[2 * pad:2 * pad + heads], (0, 0))
+
+    for distance in range(1, head_devices):
+
+        @pl.when(my_head + distance < head_devices)
+        def _():
+            pl.semaphore_wait(head_ready.at[distance - 1], 1)
 
     for away in range(1, members):
         remote(
@@ -403,6 +457,7 @@
             head=lax.rem(my_head + away, head_devices),
         ).start()
 
+    finish_keys()
     peer = {"head": lax.rem(my_head + 1, head_devices)}
     if head_devices > 1:
         passed = lat_slots.at[pl.ds(0, head_devices - 1)]
@@ -421,7 +476,7 @@
     gw_ref[...] = total
 
     passed = t_ref.at[pl.ds(0, layer - 1)]
-    remote(passed, passed, t_send, t_recv, seq=mate).wait_send()
+    remote(passed, passed, t_send, t_recv.at[0], seq=mate).wait_send()
     remote(mate_in, mate_in, mate_send, mate_recv.at[0], seq=mate).wait_send()
     passed = rs_out.at[pl.ds(0, CHIPS - 1)]
     remote(passed, passed, rs_send, rs_recv.at[0, 0], seq=mate).wait_send()
@@ -447,7 +502,8 @@
     for copy in copies:
         copy.start()
     olat[...] = glat[...]
-    ow[...] = gw[0:ow.shape[0], 0:ow.shape[1]]
+    for head in range(ow.shape[0]):
+        ow[head:head + 1] = gw[:, head * ow.shape[1]:(head + 1) * ow.shape[1]]
     for copy in copies:
         copy.wait()
 
@@ -488,7 +544,7 @@
     results = pl.pallas_call(
         functools.partial(kernel, (seq_count, dp_count, head_devices, heads)),
         out_shape=(
-            wide, wide, wide, pltpu.VMEM((rank, rows), F32), pltpu.VMEM((8, LANES), F32),
+            wide, wide, wide, pltpu.VMEM((rank, rows), F32), pltpu.VMEM((1, LANES), F32),
         ),
         in_specs=[hbm] * 8,
         scratch_shapes=[
@@ -497,6 +553,7 @@
             pltpu.VMEM((heads, rank), BF16),
             pltpu.VMEM((1, heads), F32),
             pltpu.VMEM(doc_starts.shape, jnp.int32),
+            pltpu.VMEM((LANES, rows), BF16),
             pltpu.VMEM((3 * pad, rows), F32),
             pltpu.VMEM((LANES, rows), F32),
             pltpu.VMEM((rows, LANES), F32),
@@ -512,10 +569,12 @@
             pltpu.VMEM((far, quarter, LEAD + HEAD_DIM, HEAD_DIM), F32),
             square(CHIPS, quarter), square(heads), square(2, heads),
             pltpu.VMEM((head_devices, rank, rows), F32),
-            pltpu.VMEM((members, 8, LANES), F32),
-            dma(4), dma(4), single, single, single, dma(heads), single, dma(CHIPS, CHUNKS),
+            pltpu.VMEM((members, 1, LANES), F32),
+            dma(4), dma(4), single, dma(2), single, dma(heads), single, dma(CHIPS, CHUNKS),
             dma(far), dma(far, CHUNKS), single, dma(CHIPS, CHUNKS), single, single,
             single, single, single, single,
+            pltpu.SemaphoreType.REGULAR((far,)),
+            pltpu.SemaphoreType.REGULAR((max(1, head_devices - 1),)),
         ],
         compiler_params=pltpu.CompilerParams(collective_id=0, has_side_effects=True),
         name="gated_backward",

time: 29.9 us -> 25.9 us (0.87)
  Pallas kernels: 29 us -> 25.1 us
    pallas_call x1, Pallas kernels: 27.5 us -> 23.6 us  [on_device(): pl.pallas_call(functools.partial(kernel, (seq_count, dp_count, head_devic...]
where the time goes in v3:
time: 25.9 us; the launch traced here: 25.7 us
  Pallas kernels  25.1 us (97%)
  between operations  0.64 us (2%)
    pallas_call x1, Pallas kernels, on_device(): pl.pallas_call(functools.partial(kernel, (seq_count, dp_count, head_devic...  23.6 us
    pallas_call x1, Pallas kernels, emit(): pl.pallas_call(emit_kernel, out_shape=(wide, wide, wide, jax.ShapeDtypeSt...  1.51 us

profile of v3, /device:TPU:0, one launch (start us, length us, event | category | flops | bytes accessed | tf_op | source)
XLA Modules:
  0.0 25.7 jit_solution(2780810589860448516)
XLA Ops:
  0.6 23.6 %gated_backward.1 = (bf16[256,512]{1,0:T(8,128)(2,1)S(1)}, bf16[256,512]{1,0:T(8,128)(2,1)S(1)}, bf16[256,512]{1,0:T(8,128)(2,1)S(1)}, f32[16,256]{1,0:T(8,128)S(1)}, f32[1,128]{1,0:T(1,128)S(1)}) custom-call(bf16[256,512]{1,0:T(8,128)(2,1)} %bitcast.16, bf16[256,512]{1,0:T(8,128)(2,1)} %bitcast.17, bf16[256,512]{1,0:T(8,128)(2,1)} %bitcast.18, ...), custom_call_target="tpu_custom_call" | custom-call | tf_op jit(solution)/shard_map/gated_backward/pallas_call | solution.py:544
  24.2 1.5 %emit.1 = (bf16[256,512]{1,0:T(8,128)(2,1)}, bf16[256,512]{1,0:T(8,128)(2,1)}, bf16[256,512]{1,0:T(8,128)(2,1)}, f32[16,256]{1,0:T(8,128)}, f32[4,16]{1,0:T(4,128)}) custom-call(bf16[256,512]{1,0:T(8,128)(2,1)S(1)} %get-tuple-element.15.gq, bf16[256,512]{1,0:T(8,128)(2,1)S(1)} %get-tuple-element.16.gk, bf16[256,512]{1,0:T(8,128)(2,1)S(1)} %get-tuple-element.17.gv, ...), custom_call_target="tpu_custom_call" | custom-call | tf_op jit(solution)/shard_map/emit/pallas_call | solution.py:515

commit v4 on v3

--- a/solution.py
+++ b/solution.py
@@ -230,7 +230,7 @@
     def rs_copy(target, source, i, c):
         return remote(
             rs_out.at[target, i, span(c)], rs_in.at[source, i, span(c)],
-            rs_send, rs_recv.at[source, c], seq=at_chip(target),
+            rs_send, rs_recv.at[c], seq=at_chip(target),
         )
 
     def blk_copy(distance, i, c):
@@ -242,7 +242,7 @@
     def ag_copy(target, source, i, c):
         return remote(
             ag_out.at[target, i, span(c)], state_ref.at[core, source * quarter + i, span(c)],
-            ag_send, ag_recv.at[source, c], seq=at_chip(target),
+            ag_send, ag_recv.at[source], seq=at_chip(target),
         )
 
     def back_copy(head):
@@ -264,10 +264,12 @@
             pltpu.make_async_copy(k_hbm, x_ref.at[index], load_sem.at[index]).wait()
 
     load_wait(1 - core)
-    for whose, i in order:
-        head = whose * quarter + i
-        part(1 - core, head)
-        mate_copy(head).start()
+    for first in range(0, heads, 4):
+        batch = [whose * quarter + i for whose, i in order[first:first + 4]]
+        for head in batch:
+            part(1 - core, head)
+        for head in batch:
+            mate_copy(head).start()
     load_wait(core)
     for whose, i in order:
         part(core, whose * quarter + i)
@@ -277,17 +279,19 @@
     def decay_of(index, head):
         return t_ref[index, pl.ds(head, 1), :]
 
-    for whose, i in order:
-        head = whose * quarter + i
-        keep = decay_of(PAIR * chip + 1 - core, head)
-        mate_copy(head).wait_recv()
+    def send_parts():
+        for whose, i in order:
+            mate_copy(whose * quarter + i).wait_recv()
         for c in range(CHUNKS):
-            total = keep * part_ref[core, head, span(c)] + mate_in[head, span(c)]
-            if whose is chip:
-                rs_in[chip, i, span(c)] = total
-            else:
-                rs_out[whose, i, span(c)] = total
-                rs_copy(whose, chip, i, c).start()
+            for whose, i in order:
+                head = whose * quarter + i
+                keep = decay_of(PAIR * chip + 1 - core, head)
+                total = keep * part_ref[core, head, span(c)] + mate_in[head, span(c)]
+                if whose is chip:
+                    rs_in[chip, i, span(c)] = total
+                else:
+                    rs_out[whose, i, span(c)] = total
+                    rs_copy(whose, chip, i, c).start()
 
     lane_id = lax.broadcasted_iota(jnp.int32, (rows, LANES), 1)
 
@@ -311,11 +315,14 @@
         )
         down_ref[head:head + 1] = jnp.sum(products, axis=0, keepdims=True)
 
+    passes_on = sends_to(1)
+    pl.when(passes_on)(send_parts)
     for index in range(LANES // rank):
         tiled_ref[index * rank:(index + 1) * rank] = latent_ref[...]
     cols_ref[...] = rows_ref[...].T
     for head in range(heads):
         local_head(head)
+    pl.when(jnp.logical_not(passes_on))(send_parts)
 
     def kth(k):
         return jnp.where(core == 0, k, CHIPS - 1 - k)
@@ -332,9 +339,9 @@
             pl.semaphore_wait(block_ready.at[distance - 1], 1)
 
     for c in range(CHUNKS):
+        passed = rs_in.at[pl.ds(0, CHIPS - 1), :, span(c)]
+        remote(passed, passed, rs_send, rs_recv.at[c], seq=mate).wait_recv()
         for i in range(quarter):
-            for source in others:
-                rs_copy(source, source, i, c).wait_recv()
             head = chip * quarter + i
             total = rs_in[kth(0), i, span(c)]
             for k in range(1, CHIPS):
@@ -373,15 +380,18 @@
             for target in others:
                 ag_copy(target, chip, i, c).start()
 
-    for whose, i in ((whose, i) for whose in (chip, beside, above, opposite) for i in range(quarter)):
-        head = whose * quarter + i
-        if whose is chip:
-            state_ref[core, head] = ag_out[chip, i]
-        else:
-            for c in range(CHUNKS):
-                ag_copy(whose, whose, i, c).wait_recv()
-        back_out[head] = decay_of(place, head) * state_ref[core, head] + part_ref[core, head]
-        back_copy(head).start()
+    for whose in (chip, beside, above, opposite):
+        mine = pl.ds(whose * quarter, quarter)
+        if whose is not chip:
+            remote(
+                ag_out.at[whose], state_ref.at[core, mine], ag_send, ag_recv.at[whose], seq=mate
+            ).wait_recv()
+        for i in range(quarter):
+            head = whose * quarter + i
+            if whose is chip:
+                state_ref[core, head] = ag_out[chip, i]
+            back_out[head] = decay_of(place, head) * state_ref[core, head] + part_ref[core, head]
+            back_copy(head).start()
 
     def finish_state():
         for head in range(heads):
@@ -479,9 +489,9 @@
     remote(passed, passed, t_send, t_recv.at[0], seq=mate).wait_send()
     remote(mate_in, mate_in, mate_send, mate_recv.at[0], seq=mate).wait_send()
     passed = rs_out.at[pl.ds(0, CHIPS - 1)]
-    remote(passed, passed, rs_send, rs_recv.at[0, 0], seq=mate).wait_send()
+    remote(passed, passed, rs_send, rs_recv.at[0], seq=mate).wait_send()
     passed = ag_out.at[pl.ds(0, CHIPS - 1)]
-    remote(passed, passed, ag_send, ag_recv.at[0, 0], seq=mate).wait_send()
+    remote(passed, passed, ag_send, ag_recv.at[0], seq=mate).wait_send()
     remote(back_out, back_out, back_send, back_recv, seq=mate).wait_send()
     for distance in range(1, blocks):
         pl.when(sends_to(distance))(
@@ -494,18 +504,13 @@
     sums.wait_send()
 
 
-def emit_kernel(gq, gk, gv, glat, gw, oq, ok, ov, olat, ow, sems):
-    copies = [
-        pltpu.make_async_copy(source, target, sems.at[index])
-        for index, (source, target) in enumerate(((gq, oq), (gk, ok), (gv, ov)))
-    ]
-    for copy in copies:
-        copy.start()
+def emit_kernel(gq, gk, gv, glat, gw, oq, ok, ov, olat, ow):
+    oq[...] = gq[...]
+    ok[...] = gk[...]
+    ov[...] = gv[...]
     olat[...] = glat[...]
     for head in range(ow.shape[0]):
         ow[head:head + 1] = gw[:, head * ow.shape[1]:(head + 1) * ow.shape[1]]
-    for copy in copies:
-        copy.wait()
 
 
 def emit(results, rows, width, rank, heads):
@@ -519,8 +524,8 @@
             jax.ShapeDtypeStruct((rank, rows), F32), jax.ShapeDtypeStruct((heads, rank), F32),
         ),
         in_specs=[vmem] * 5,
-        out_specs=(hbm, hbm, hbm, vmem, vmem),
-        scratch_shapes=[pltpu.SemaphoreType.DMA((3,))],
+        out_specs=(vmem,) * 5,
+
         name="emit",
     )(*(pltpu.with_memory_space_constraint(result, pltpu.VMEM) for result in results))
 
@@ -570,8 +575,8 @@
             square(CHIPS, quarter), square(heads), square(2, heads),
             pltpu.VMEM((head_devices, rank, rows), F32),
             pltpu.VMEM((members, 1, LANES), F32),
-            dma(4), dma(4), single, dma(2), single, dma(heads), single, dma(CHIPS, CHUNKS),
-            dma(far), dma(far, CHUNKS), single, dma(CHIPS, CHUNKS), single, single,
+            dma(4), dma(4), single, dma(2), single, dma(heads), single, dma(CHUNKS),
+            dma(far), dma(far, CHUNKS), single, dma(CHIPS), single, single,
             single, single, single, single,
             pltpu.SemaphoreType.REGULAR((far,)),
             pltpu.SemaphoreType.REGULAR((max(1, head_devices - 1),)),

time: 25.9 us -> 24.6 us (0.950)
  Pallas kernels: 25.1 us -> 23.7 us
    pallas_call x1, Pallas kernels: 23.6 us -> 22.8 us  [on_device(): pl.pallas_call(functools.partial(kernel, (seq_count, dp_count, head_devic...]
    pallas_call x1, Pallas kernels: 1.51 us -> 0.9 us  [emit(): pl.pallas_call(emit_kernel, out_shape=(wide, wide, wide, jax.ShapeDtypeSt...]
where the time goes in v4:
time: 24.6 us; the launch traced here: 24.3 us
  Pallas kernels  23.7 us (96%)
  between operations  0.64 us (3%)
    pallas_call x1, Pallas kernels, on_device(): pl.pallas_call(functools.partial(kernel, (seq_count, dp_count, head_devic...  22.8 us
    pallas_call x1, Pallas kernels, emit(): pl.pallas_call(emit_kernel, out_shape=(wide, wide, wide, jax.ShapeDtypeSt...  0.9 us

profile of v4, /device:TPU:0, one launch (start us, length us, event | category | flops | bytes accessed | tf_op | source)
XLA Modules:
  0.0 24.3 jit_solution(2382716256295335425)
XLA Ops:
  0.6 22.8 %gated_backward.1 = (bf16[256,512]{1,0:T(8,128)(2,1)S(1)}, bf16[256,512]{1,0:T(8,128)(2,1)S(1)}, bf16[256,512]{1,0:T(8,128)(2,1)S(1)}, f32[16,256]{1,0:T(8,128)S(1)}, f32[1,128]{1,0:T(1,128)S(1)}) custom-call(bf16[256,512]{1,0:T(8,128)(2,1)} %bitcast.16, bf16[256,512]{1,0:T(8,128)(2,1)} %bitcast.17, bf16[256,512]{1,0:T(8,128)(2,1)} %bitcast.18, ...), custom_call_target="tpu_custom_call" | custom-call | tf_op jit(solution)/shard_map/gated_backward/pallas_call | solution.py:549
  23.4 0.9 %emit.1 = (bf16[256,512]{1,0:T(8,128)(2,1)}, bf16[256,512]{1,0:T(8,128)(2,1)}, bf16[256,512]{1,0:T(8,128)(2,1)}, f32[16,256]{1,0:T(8,128)}, f32[4,16]{1,0:T(4,128)}) custom-call(bf16[256,512]{1,0:T(8,128)(2,1)S(1)} %get-tuple-element.15.gq, bf16[256,512]{1,0:T(8,128)(2,1)S(1)} %get-tuple-element.16.gk, bf16[256,512]{1,0:T(8,128)(2,1)S(1)} %get-tuple-element.17.gv, ...), custom_call_target="tpu_custom_call" | custom-call | tf_op jit(solution)/shard_map/emit/pallas_call | solution.py:520

commit v5 on v4

--- a/solution.py
+++ b/solution.py
@@ -44,7 +44,7 @@
     k_hbm, q_hbm, v_hbm, g_hbm, latent_hbm, weight_hbm, bias_hbm, bounds_hbm,
     gq_ref, gk_ref, gv_ref, glat_ref, gw_ref,
     x_ref, latent_ref, weight_ref, bias_ref, bounds_ref,
-    tiled_ref, stack_ref, rows_ref, cols_ref, upto_ref, iq_ref, ik_ref, iv_ref, flow_ref, down_ref,
+    tiled_ref, stack_ref, rows_ref, cols_ref, upto_ref, iq_ref, ik_ref, iv_ref, left_ref, value_ref, base_ref, through_ref,
     t_ref, part_ref, mate_in, rs_out, rs_in, blk_out, blk_in, ag_out, back_out, state_ref,
     lat_slots, gw_slots,
     load_sem, small_sem, t_send, t_recv, mate_send, mate_recv, rs_send, rs_recv,
@@ -144,7 +144,6 @@
     upto_ref[...] = (row_id <= col_id).astype(F32).astype(BF16)
     stack_ref[...] = jnp.zeros_like(stack_ref)
     rows_ref[...] = jnp.zeros_like(rows_ref)
-    flow_ref[...] = jnp.zeros_like(flow_ref)
 
     def stacked(tensor):
         for index, piece in enumerate(thirds(tensor)):
@@ -254,8 +253,9 @@
 
     def part(way, head):
         lanes = pl.ds(pl.multiple_of(head * HEAD_DIM, HEAD_DIM), HEAD_DIM)
-        turned = x_ref[way, :, lanes].astype(F32).T
-        upper, lower = halves(turned * rows_ref[pl.ds(way * heads + head, 1)])
+        turned = x_ref[way, :, lanes].T
+        left_ref[way, head] = turned
+        upper, lower = halves(turned.astype(F32) * rows_ref[pl.ds(way * heads + head, 1)])
         right = x_ref[2 + way, :, lanes]
         part_ref[way, head] = dot(upper, right, (1, 0)) + dot(lower, right, (1, 0))
 
@@ -281,16 +281,19 @@
 
     def send_parts():
         for whose, i in order:
-            mate_copy(whose * quarter + i).wait_recv()
-        for c in range(CHUNKS):
-            for whose, i in order:
-                head = whose * quarter + i
-                keep = decay_of(PAIR * chip + 1 - core, head)
-                total = keep * part_ref[core, head, span(c)] + mate_in[head, span(c)]
-                if whose is chip:
-                    rs_in[chip, i, span(c)] = total
-                else:
-                    rs_out[whose, i, span(c)] = total
+            head = whose * quarter + i
+            keep = decay_of(PAIR * chip + 1 - core, head)
+            mate_copy(head).wait_recv()
+            total = keep * part_ref[core, head] + mate_in[head]
+            if whose is chip:
+                rs_in[chip, i] = total
+            else:
+                rs_out[whose, i] = total
+                for c in range(CHUNKS // 2):
+                    rs_copy(whose, chip, i, c).start()
+        for whose, i in order:
+            if whose is not chip:
+                for c in range(CHUNKS // 2, CHUNKS):
                     rs_copy(whose, chip, i, c).start()
 
     lane_id = lax.broadcasted_iota(jnp.int32, (rows, LANES), 1)
@@ -310,19 +313,23 @@
         iv_ref[:, lanes] = dot(scores.astype(BF16), grad, (0, 0))
         iq_ref[:, lanes] = dot(weighted, key, (1, 0))
         ik_ref[:, lanes] = dot(weighted, query, (0, 0))
-        flow_ref[...] += jnp.where(
-            lane_id == head, jnp.sum(products, axis=1, keepdims=True), 0.0
-        )
-        down_ref[head:head + 1] = jnp.sum(products, axis=0, keepdims=True)
+        flows.append(jnp.sum(products, axis=1, keepdims=True))
+        base_ref[head:head + 1] = jnp.sum(products, axis=0, keepdims=True)
 
     passes_on = sends_to(1)
     pl.when(passes_on)(send_parts)
     for index in range(LANES // rank):
         tiled_ref[index * rank:(index + 1) * rank] = latent_ref[...]
     cols_ref[...] = rows_ref[...].T
+    flows = []
     for head in range(heads):
         local_head(head)
     pl.when(jnp.logical_not(passes_on))(send_parts)
+    gathered = jnp.zeros((rows, LANES), F32)
+    for head in range(heads):
+        gathered = jnp.where(lane_id == head, flows[head], gathered)
+        value_ref[head] = x_ref[2, :, head_lanes(head)].T
+    base_ref[0:heads] = gathered.T[0:heads] - base_ref[0:heads]
 
     def kth(k):
         return jnp.where(core == 0, k, CHIPS - 1 - k)
@@ -393,49 +400,52 @@
             back_out[head] = decay_of(place, head) * state_ref[core, head] + part_ref[core, head]
             back_copy(head).start()
 
-    def finish_state():
+    def state_rows():
+        for head in range(heads):
+            upper, lower = halves(state_ref[0, head])
+            grad = x_ref[3, :, head_lanes(head)]
+            carried = dot(upper, grad, (1, 1)) + dot(lower, grad, (1, 1))
+            inflow = jnp.sum(carried * left_ref[1, head].astype(F32), axis=0, keepdims=True)
+            through_ref[head:head + 1] = inflow * rows_ref[heads + head:heads + head + 1]
+
+    def back_rows():
+        for head in range(heads):
+            upper, lower = halves(state_ref[1, head])
+            key = x_ref[0, :, head_lanes(head)]
+            carried = dot(upper, key, (0, 1)) + dot(lower, key, (0, 1))
+            outflow = jnp.sum(carried * value_ref[head].astype(F32), axis=0, keepdims=True)
+            through_ref[pad + head:pad + head + 1] = outflow * rows_ref[head:head + 1]
+
+    def finish_heads():
         for head in range(heads):
             lanes = head_lanes(head)
-            query, grad = x_ref[1, :, lanes], x_ref[3, :, lanes]
+            key, query, value, grad = (x_ref[index, :, lanes] for index in range(4))
+            enter, leave = column(heads + head), column(head)
             upper, lower = halves(state_ref[0, head])
-            carried = (dot(grad, upper, (1, 1)) + dot(grad, lower, (1, 1))) * column(heads + head)
+            carried = (dot(grad, upper, (1, 1)) + dot(grad, lower, (1, 1))) * enter
             gq_ref[:, lanes] = (iq_ref[:, lanes] + carried).astype(BF16)
-            inflow = jnp.sum(query.astype(F32) * carried, axis=1, keepdims=True)
-            flow_ref[...] += jnp.where(lane_id == head, inflow, 0.0)
-
-    def finish_back():
-        for head in range(heads):
-            lanes = head_lanes(head)
-            key, value = x_ref[0, :, lanes], x_ref[2, :, lanes]
             upper, lower = halves(state_ref[1, head])
-            leave = column(head)
             carried = (dot(key, upper, (1, 0)) + dot(key, lower, (1, 0))) * leave
             gv_ref[:, lanes] = (iv_ref[:, lanes] + carried).astype(BF16)
-            outflow = jnp.sum(value.astype(F32) * carried, axis=1, keepdims=True)
-            flow_ref[...] -= jnp.where(lane_id == head, outflow, 0.0)
-            total = jnp.sum(outflow, axis=0, keepdims=True)
-            down_ref[heads + head:heads + head + 1] = jnp.broadcast_to(total, (1, rows))
-
-    def finish_keys():
-        for head in range(heads):
-            lanes = head_lanes(head)
-            carried = dot(x_ref[2, :, lanes], state_ref[1, head].astype(BF16), (1, 1)) * column(head)
+            carried = dot(value, upper, (1, 1)) * leave
             gk_ref[:, lanes] = (ik_ref[:, lanes] + carried).astype(BF16)
 
-    pl.when(core == 0)(finish_state)
-    pl.when(core == 1)(finish_back)
+    pl.when(core == 0)(state_rows)
+    pl.when(core == 1)(back_rows)
     remote(back_out, state_ref.at[1 - core], back_send, back_recv, seq=mate).wait_recv()
-    pl.when(core == 0)(finish_back)
-    pl.when(core == 1)(finish_state)
-
-    turned = flow_ref[...].T[0:heads]
+    pl.when(core == 0)(back_rows)
+    pl.when(core == 1)(state_rows)
+
     wholes = [
         jnp.sum(jnp.sum(state_ref[0, head] * state_ref[1, head], axis=0, keepdims=True), axis=1, keepdims=True)
         for head in range(heads)
     ]
-    end_term = through * jnp.concatenate(wholes, axis=0) + down_ref[heads:2 * heads]
+    inflow, outflow = through_ref[0:heads], through_ref[pad:pad + heads]
+    end_term = through * jnp.concatenate(wholes, axis=0) + jnp.sum(outflow, axis=1, keepdims=True)
     row_lane = lax.broadcasted_iota(jnp.int32, (heads, rows), 1)
-    grad_cumul = turned - down_ref[0:heads] + jnp.where(row_lane == rows - 1, end_term, 0.0)
+    grad_cumul = base_ref[0:heads] + (inflow - outflow) + jnp.where(
+        row_lane == rows - 1, end_term, 0.0
+    )
     grad_log = unstacked(dot(stacked(grad_cumul), upto_ref[...], (1, 1)))
     grad_gate = grad_log * (1.0 / (1.0 + jnp.exp(gate_rows))) / 16.0
     pieces = stacked(grad_gate)
@@ -467,7 +477,21 @@
             head=lax.rem(my_head + away, head_devices),
         ).start()
 
-    finish_keys()
+    finish_heads()
+    passed = t_ref.at[pl.ds(0, layer - 1)]
+    remote(passed, passed, t_send, t_recv.at[0], seq=mate).wait_send()
+    remote(mate_in, mate_in, mate_send, mate_recv.at[0], seq=mate).wait_send()
+    passed = rs_out.at[pl.ds(0, CHIPS - 1)]
+    remote(passed, passed, rs_send, rs_recv.at[0], seq=mate).wait_send()
+    passed = ag_out.at[pl.ds(0, CHIPS - 1)]
+    remote(passed, passed, ag_send, ag_recv.at[0], seq=mate).wait_send()
+    remote(back_out, back_out, back_send, back_recv, seq=mate).wait_send()
+    for distance in range(1, blocks):
+        pl.when(sends_to(distance))(
+            remote(
+                blk_out, blk_out, blk_send.at[distance - 1], blk_recv.at[0, 0], seq=mate
+            ).wait_send
+        )
     peer = {"head": lax.rem(my_head + 1, head_devices)}
     if head_devices > 1:
         passed = lat_slots.at[pl.ds(0, head_devices - 1)]
@@ -485,20 +509,6 @@
         total = total + gw_slots[slot]
     gw_ref[...] = total
 
-    passed = t_ref.at[pl.ds(0, layer - 1)]
-    remote(passed, passed, t_send, t_recv.at[0], seq=mate).wait_send()
-    remote(mate_in, mate_in, mate_send, mate_recv.at[0], seq=mate).wait_send()
-    passed = rs_out.at[pl.ds(0, CHIPS - 1)]
-    remote(passed, passed, rs_send, rs_recv.at[0], seq=mate).wait_send()
-    passed = ag_out.at[pl.ds(0, CHIPS - 1)]
-    remote(passed, passed, ag_send, ag_recv.at[0], seq=mate).wait_send()
-    remote(back_out, back_out, back_send, back_recv, seq=mate).wait_send()
-    for distance in range(1, blocks):
-        pl.when(sends_to(distance))(
-            remote(
-                blk_out, blk_out, blk_send.at[distance - 1], blk_recv.at[0, 0], seq=mate
-            ).wait_send
-        )
     if head_devices > 1:
         lats.wait_send()
     sums.wait_send()
@@ -566,7 +576,9 @@
             pltpu.VMEM((rows, width), F32),
             pltpu.VMEM((rows, width), F32),
             pltpu.VMEM((rows, width), F32),
-            pltpu.VMEM((rows, LANES), F32),
+            pltpu.VMEM((2, heads, HEAD_DIM, rows), BF16),
+            pltpu.VMEM((heads, HEAD_DIM, rows), BF16),
+            pltpu.VMEM((pad, rows), F32),
             pltpu.VMEM((2 * pad, rows), F32),
             pltpu.VMEM((layer, 8, LANES), F32),
             square(2, heads), square(heads), square(CHIPS, quarter), square(CHIPS, quarter),

time: 24.6 us -> 23.7 us (0.963)
  Pallas kernels: 23.7 us -> 22.8 us
    pallas_call x1, Pallas kernels: 22.8 us -> 21.9 us  [on_device(): pl.pallas_call(functools.partial(kernel, (seq_count, dp_count, head_devic...]
where the time goes in v5:
time: 23.7 us; the launch traced here: 23.4 us
  Pallas kernels  22.8 us (96%)
  between operations  0.64 us (3%)
    pallas_call x1, Pallas kernels, on_device(): pl.pallas_call(functools.partial(kernel, (seq_count, dp_count, head_devic...  21.9 us
    pallas_call x1, Pallas kernels, emit(): pl.pallas_call(emit_kernel, out_shape=(wide, wide, wide, jax.ShapeDtypeSt...  0.9 us

profile of v5, /device:TPU:0, one launch (start us, length us, event | category | flops | bytes accessed | tf_op | source)
XLA Modules:
  0.0 23.4 jit_solution(13297730160477360665)
XLA Ops:
  0.6 21.9 %gated_backward.1 = (bf16[256,512]{1,0:T(8,128)(2,1)S(1)}, bf16[256,512]{1,0:T(8,128)(2,1)S(1)}, bf16[256,512]{1,0:T(8,128)(2,1)S(1)}, f32[16,256]{1,0:T(8,128)S(1)}, f32[1,128]{1,0:T(1,128)S(1)}) custom-call(bf16[256,512]{1,0:T(8,128)(2,1)} %bitcast.16, bf16[256,512]{1,0:T(8,128)(2,1)} %bitcast.17, bf16[256,512]{1,0:T(8,128)(2,1)} %bitcast.18, ...), custom_call_target="tpu_custom_call" | custom-call | tf_op jit(solution)/shard_map/gated_backward/pallas_call | solution.py:559
  22.5 0.9 %emit.1 = (bf16[256,512]{1,0:T(8,128)(2,1)}, bf16[256,512]{1,0:T(8,128)(2,1)}, bf16[256,512]{1,0:T(8,128)(2,1)}, f32[16,256]{1,0:T(8,128)}, f32[4,16]{1,0:T(4,128)}) custom-call(bf16[256,512]{1,0:T(8,128)(2,1)S(1)} %get-tuple-element.15.gq, bf16[256,512]{1,0:T(8,128)(2,1)S(1)} %get-tuple-element.16.gk, bf16[256,512]{1,0:T(8,128)(2,1)S(1)} %get-tuple-element.17.gv, ...), custom_call_target="tpu_custom_call" | custom-call | tf_op jit(solution)/shard_map/emit/pallas_call | solution.py:530

commit v6 on v5

--- a/solution.py
+++ b/solution.py
@@ -107,16 +107,6 @@
     for copy in small:
         copy.start()
 
-    @pl.when(core == 0)
-    def _():
-        for index in (1, 3, 0, 2):
-            loads[index].start()
-
-    @pl.when(core == 1)
-    def _():
-        for index in (0, 2, 1, 3):
-            loads[index].start()
-
     barrier = pltpu.get_barrier_semaphore()
     greeted = layer - 1 + seq_count * (dp_count - 1)
     for away in range(1, layer):
@@ -138,6 +128,16 @@
             greet(barrier, head=my_head + distance)
 
         greeted = greeted + jnp.where(my_head >= distance, 1, 0)
+
+    @pl.when(core == 0)
+    def _():
+        for index in (1, 3, 0, 2):
+            loads[index].start()
+
+    @pl.when(core == 1)
+    def _():
+        for index in (0, 2, 1, 3):
+            loads[index].start()
 
     row_id = lax.broadcasted_iota(jnp.int32, (rows, rows), 0)
     col_id = lax.broadcasted_iota(jnp.int32, (rows, rows), 1)
@@ -176,6 +176,7 @@
     rows_ref[heads:2 * heads] = jnp.where(doc_row == 0.0, jnp.exp(cumul), 0.0) * scaling
     rows_ref[2 * heads:3 * heads] = cumul
     rows_ref[3 * heads:3 * heads + 8] = docs
+    through_ref[2 * pad:2 * pad + heads] = (1.0 / (1.0 + jnp.exp(gate_rows))) / 16.0
     t_ref[place, 0:heads] = jnp.broadcast_to(through, (heads, LANES))
 
     def column(index):
@@ -211,9 +212,6 @@
         )
 
     decay_copy(mate, place).start()
-    for whose in others:
-        for peer in range(PAIR):
-            decay_copy(group + whose * PAIR + peer, place).start()
 
     def mate_copy(head):
         return remote(
@@ -270,6 +268,9 @@
             part(1 - core, head)
         for head in batch:
             mate_copy(head).start()
+    for whose in others:
+        for peer in range(PAIR):
+            decay_copy(group + whose * PAIR + peer, place).start()
     load_wait(core)
     for whose, i in order:
         part(core, whose * quarter + i)
@@ -447,7 +448,7 @@
         row_lane == rows - 1, end_term, 0.0
     )
     grad_log = unstacked(dot(stacked(grad_cumul), upto_ref[...], (1, 1)))
-    grad_gate = grad_log * (1.0 / (1.0 + jnp.exp(gate_rows))) / 16.0
+    grad_gate = grad_log * through_ref[2 * pad:2 * pad + heads]
     pieces = stacked(grad_gate)
     spread = unstacked(dot(pieces, tiled_ref[...], (1, 1)))
     lane = lax.broadcasted_iota(jnp.int32, (heads, LANES), 1)
@@ -455,22 +456,22 @@
     gw_slots[flat] = jnp.sum(
         jnp.where(lax.div(lane, rank) == owner, spread, 0.0), axis=0, keepdims=True
     )
-    weight = weight_ref[...]
-    lat_slots[my_head] = (
-        dot(weight, pieces[0:heads], (0, 0)) + dot(weight, pieces[pad:pad + heads], (0, 0))
-    ) + dot(weight, pieces[2 * pad:2 * pad + heads], (0, 0))
-
-    for distance in range(1, head_devices):
-
-        @pl.when(my_head + distance < head_devices)
-        def _():
-            pl.semaphore_wait(head_ready.at[distance - 1], 1)
-
     for away in range(1, members):
         remote(
             gw_slots.at[flat], gw_slots.at[flat], gw_send, gw_recv,
             **member(lax.rem(flat + away, members)),
         ).start()
+    weight = weight_ref[...]
+    lat_slots[my_head] = (
+        dot(weight, pieces[0:heads], (0, 0)) + dot(weight, pieces[pad:pad + heads], (0, 0))
+    ) + dot(weight, pieces[2 * pad:2 * pad + heads], (0, 0))
+
+    for distance in range(1, head_devices):
+
+        @pl.when(my_head + distance < head_devices)
+        def _():
+            pl.semaphore_wait(head_ready.at[distance - 1], 1)
+
     for away in range(1, head_devices):
         remote(
             lat_slots.at[my_head], lat_slots.at[my_head], lat_send, lat_recv,
@@ -579,7 +580,7 @@
             pltpu.VMEM((2, heads, HEAD_DIM, rows), BF16),
             pltpu.VMEM((heads, HEAD_DIM, rows), BF16),
             pltpu.VMEM((pad, rows), F32),
-            pltpu.VMEM((2 * pad, rows), F32),
+            pltpu.VMEM((3 * pad, rows), F32),
             pltpu.VMEM((layer, 8, LANES), F32),
             square(2, heads), square(heads), square(CHIPS, quarter), square(CHIPS, quarter),
             pltpu.VMEM((quarter, LEAD + HEAD_DIM, HEAD_DIM), F32),

time: 23.7 us -> 23.6 us (level)
  no operation moved by 1% of the time
where the time goes in v6:
time: 23.6 us; the launch traced here: 23.4 us
  Pallas kernels  22.8 us (97%)
  between operations  0.64 us (3%)
    pallas_call x1, Pallas kernels, on_device(): pl.pallas_call(functools.partial(kernel, (seq_count, dp_count, head_devic...  21.9 us
    pallas_call x1, Pallas kernels, emit(): pl.pallas_call(emit_kernel, out_shape=(wide, wide, wide, jax.ShapeDtypeSt...  0.9 us

profile of v6, /device:TPU:0, one launch (start us, length us, event | category | flops | bytes accessed | tf_op | source)
XLA Modules:
  0.0 23.4 jit_solution(7613279167647144714)
XLA Ops:
  0.6 21.9 %gated_backward.1 = (bf16[256,512]{1,0:T(8,128)(2,1)S(1)}, bf16[256,512]{1,0:T(8,128)(2,1)S(1)}, bf16[256,512]{1,0:T(8,128)(2,1)S(1)}, f32[16,256]{1,0:T(8,128)S(1)}, f32[1,128]{1,0:T(1,128)S(1)}) custom-call(bf16[256,512]{1,0:T(8,128)(2,1)} %bitcast.16, bf16[256,512]{1,0:T(8,128)(2,1)} %bitcast.17, bf16[256,512]{1,0:T(8,128)(2,1)} %bitcast.18, ...), custom_call_target="tpu_custom_call" | custom-call | tf_op jit(solution)/shard_map/gated_backward/pallas_call | solution.py:560
  22.5 0.9 %emit.1 = (bf16[256,512]{1,0:T(8,128)(2,1)}, bf16[256,512]{1,0:T(8,128)(2,1)}, bf16[256,512]{1,0:T(8,128)(2,1)}, f32[16,256]{1,0:T(8,128)}, f32[4,16]{1,0:T(4,128)}) custom-call(bf16[256,512]{1,0:T(8,128)(2,1)S(1)} %get-tuple-element.15.gq, bf16[256,512]{1,0:T(8,128)(2,1)S(1)} %get-tuple-element.16.gk, bf16[256,512]{1,0:T(8,128)(2,1)S(1)} %get-tuple-element.17.gv, ...), custom_call_target="tpu_custom_call" | custom-call | tf_op jit(solution)/shard_map/emit/pallas_call | solution.py:531

commit v7 on v6

--- a/solution.py
+++ b/solution.py
@@ -335,6 +335,10 @@
     def kth(k):
         return jnp.where(core == 0, k, CHIPS - 1 - k)
 
+    def is_needed(target):
+        begins = jnp.where(core == 0, block == 0, block == blocks - 1)
+        return jnp.logical_not(begins & (target == kth(0)))
+
     def chip_decay(index, head):
         return decay_of(PAIR * index, head) * decay_of(PAIR * index + 1, head)
 
@@ -386,14 +390,20 @@
                 if k < CHIPS - 1:
                     entering = chip_decay(kth(k), head) * entering + rs_in[kth(k), i, span(c)]
             for target in others:
-                ag_copy(target, chip, i, c).start()
+                pl.when(is_needed(target))(ag_copy(target, chip, i, c).start)
 
     for whose in (chip, beside, above, opposite):
         mine = pl.ds(whose * quarter, quarter)
         if whose is not chip:
-            remote(
+            arriving = remote(
                 ag_out.at[whose], state_ref.at[core, mine], ag_send, ag_recv.at[whose], seq=mate
-            ).wait_recv()
+            )
+            pl.when(is_needed(chip))(arriving.wait_recv)
+
+            @pl.when(jnp.logical_not(is_needed(chip)))
+            def _():
+                state_ref[core, mine] = jnp.zeros((quarter, HEAD_DIM, HEAD_DIM), F32)
+
         for i in range(quarter):
             head = whose * quarter + i
             if whose is chip:
@@ -484,8 +494,12 @@
     remote(mate_in, mate_in, mate_send, mate_recv.at[0], seq=mate).wait_send()
     passed = rs_out.at[pl.ds(0, CHIPS - 1)]
     remote(passed, passed, rs_send, rs_recv.at[0], seq=mate).wait_send()
-    passed = ag_out.at[pl.ds(0, CHIPS - 1)]
-    remote(passed, passed, ag_send, ag_recv.at[0], seq=mate).wait_send()
+    for target in others:
+        pl.when(is_needed(target))(
+            remote(
+                ag_out.at[target], ag_out.at[target], ag_send, ag_recv.at[0], seq=mate
+            ).wait_send
+        )
     remote(back_out, back_out, back_send, back_recv, seq=mate).wait_send()
     for distance in range(1, blocks):
         pl.when(sends_to(distance))(

time: 23.6 us -> 23.6 us (level)
  no operation moved by 1% of the time
where the time goes in v7:
time: 23.6 us; the launch traced here: 23.4 us
  Pallas kernels  22.8 us (97%)
  between operations  0.64 us (3%)
    pallas_call x1, Pallas kernels, on_device(): pl.pallas_call(functools.partial(kernel, (seq_count, dp_count, head_devic...  21.9 us
    pallas_call x1, Pallas kernels, emit(): pl.pallas_call(emit_kernel, out_shape=(wide, wide, wide, jax.ShapeDtypeSt...  0.9 us

profile of v7, /device:TPU:0, one launch (start us, length us, event | category | flops | bytes accessed | tf_op | source)
XLA Modules:
  0.0 23.4 jit_solution(8524796459221093745)
XLA Ops:
  0.6 21.9 %gated_backward.1 = (bf16[256,512]{1,0:T(8,128)(2,1)S(1)}, bf16[256,512]{1,0:T(8,128)(2,1)S(1)}, bf16[256,512]{1,0:T(8,128)(2,1)S(1)}, f32[16,256]{1,0:T(8,128)S(1)}, f32[1,128]{1,0:T(1,128)S(1)}) custom-call(bf16[256,512]{1,0:T(8,128)(2,1)} %bitcast.16, bf16[256,512]{1,0:T(8,128)(2,1)} %bitcast.17, bf16[256,512]{1,0:T(8,128)(2,1)} %bitcast.18, ...), custom_call_target="tpu_custom_call" | custom-call | tf_op jit(solution)/shard_map/gated_backward/pallas_call | solution.py:574
  22.5 0.9 %emit.1 = (bf16[256,512]{1,0:T(8,128)(2,1)}, bf16[256,512]{1,0:T(8,128)(2,1)}, bf16[256,512]{1,0:T(8,128)(2,1)}, f32[16,256]{1,0:T(8,128)}, f32[4,16]{1,0:T(4,128)}) custom-call(bf16[256,512]{1,0:T(8,128)(2,1)S(1)} %get-tuple-element.15.gq, bf16[256,512]{1,0:T(8,128)(2,1)S(1)} %get-tuple-element.16.gk, bf16[256,512]{1,0:T(8,128)(2,1)S(1)} %get-tuple-element.17.gv, ...), custom_call_target="tpu_custom_call" | custom-call | tf_op jit(solution)/shard_map/emit/pallas_call | solution.py:545
